TPU v7x, 32 devices: a whole 2x2x4 slice. The times are simulated.
32 devices in a mesh: row: 4 (over z), col: 2 (over x), pole: 4 (over y, core).
Axes of the slice: x: 2, y: 2, z: 4, core: 2. Of those that a mesh axis runs over, the one named last changes fastest.
Arguments:
- window: bfloat16 [4, 8192, 8192], P('pole', 'col', 'row'), may hold values from -6 to 6
- panels: bfloat16 [4, 2, 8192, 256], P('pole', 'col', 'row'), may hold values from -0.0625 to 0.0625
- row_map: int32 [3, 8192], P(None, 'row'), may hold values from 0 to 8191, as said below
- panel_root: int32 [4, 3], P('pole'), may hold values from 0 to 1
- upper_blocks: bfloat16 [4, 3, 256, 256], P('pole', None, 'row'), may hold values from -0.375 to 0.375
- diag_inverse: float32 [4, 3, 256, 256], P('pole', None, 'row'), may hold values from -6 to 6
- weights: float32 [4], replicated, may hold values from 0.25 to 1
- pole_order: int32 [4], P('pole'), may hold values from 0 to 3, each once
Outputs:
- inv_columns: float32 [3, 2, 4096, 256], P(None, 'col', ('row', 'pole'))
- inv_diag: float32 [3, 256, 256], P(None, ('row', 'pole'))
Inputs may be any that keep to these rules, and one draw needn't show every extreme that they name: row_map[k] permutes the positions inside each aligned group of 1024 consecutive positions. `pole_order`: each of the 4 poles appears once.
All inputs are finite; a program needn't handle non-finite values.
Results may differ from a plain program's by a relative error of at most 0.0003.
Values may be sent and summed in bfloat16 or wider, within the bound.
A program may use at most 128 MiB of HBM per device.

v0:
```python
import jax
import jax.numpy as jnp
from jax import lax
from jax.experimental import pallas as pl
from jax.experimental.pallas import tpu as pltpu
from jax.sharding import PartitionSpec as P


NS = 3
CHUNKS = 2


def precise(left, right):
    return jnp.dot(left, right, precision=lax.Precision.HIGHEST, preferred_element_type=jnp.float32)


def pair_index(current, earlier):
    return current * (current - 1) // 2 + earlier


def split(value):
    high = value.astype(jnp.bfloat16)
    return high, (value - high.astype(jnp.float32)).astype(jnp.bfloat16)


def pick(stacked, index, axis=0):
    return lax.dynamic_index_in_dim(stacked, index, axis, keepdims=False)


def swap(block, axis_name, bit):
    size = lax.axis_size(axis_name)
    return lax.ppermute(block, axis_name, [(i, i ^ bit) for i in range(size)])


def shift(block, axis_name, distance):
    size = lax.axis_size(axis_name)
    return lax.ppermute(block, axis_name, [(i, (i + distance) % size) for i in range(size)])


def encode(value):
    top = jnp.maximum(jnp.max(jnp.abs(value), axis=-1), 1e-30)
    return jnp.round(value * (32000.0 / top)[..., None]).astype(jnp.int16), top


def decode(code, top):
    return code.astype(jnp.float32) * (top * (1.0 / 32000.0))[..., None]


def halving_sum(blocks, axis_name, bit):
    size = lax.axis_size(axis_name)
    index = lax.axis_index(axis_name)
    while bit < size:
        side = (index // bit) % 2
        paired = blocks.reshape((blocks.shape[0], blocks.shape[1] // 2, 2) + blocks.shape[2:])
        blocks = pick(paired, side, 2) + swap(pick(paired, 1 - side, 2), axis_name, bit)
        bit *= 2
    return blocks[:, 0]


def shift_sum(blocks, axis_name):
    size = lax.axis_size(axis_name)
    index = lax.axis_index(axis_name)
    total = pick(blocks, index)
    arrived = []
    for distance in range(1, size):
        arrived.append(shift(pick(blocks, (index + distance) % size), axis_name, distance))
    return sum(arrived, total)


def coded_sum(blocks, axis_name):
    size = lax.axis_size(axis_name)
    index = lax.axis_index(axis_name)
    total = pick(blocks, index)
    code, top = encode(blocks)
    arrived = []
    for distance in range(1, size):
        at = (index + distance) % size
        sent = shift(pick(code, at), axis_name, distance)
        arrived.append(decode(sent, shift(pick(top, at), axis_name, distance)))
    return sum(arrived, total)


def shift_gather(block, axis_name):
    size = lax.axis_size(axis_name)
    blocks = [block]
    for distance in range(1, size):
        blocks.append(shift(block, axis_name, distance))
    return blocks


def reorder_kernel(slab_ref, map_ref, rows_ref, out_ref):
    size = rows_ref.shape[2]
    chosen = lax.broadcasted_iota(jnp.int32, (size, size), 0) == map_ref[0, 0]
    out_ref[...] = lax.dot_general(
        jnp.where(chosen, 1.0, 0.0).astype(rows_ref.dtype),
        rows_ref[0, 0],
        (((0,), (0,)), ((), ())),
        preferred_element_type=jnp.float32,
    ).astype(out_ref.dtype)


def reorder(slab_index, maps, sources):
    _, groups, group, width = sources.shape
    return pl.pallas_call(
        reorder_kernel,
        out_shape=jax.ShapeDtypeStruct((groups * group, NS * width), sources.dtype),
        grid_spec=pltpu.PrefetchScalarGridSpec(
            num_scalar_prefetch=1,
            grid=(groups, NS),
            in_specs=[
                pl.BlockSpec((1, 1, 1, group), lambda a, k, slabs: (a, k, 0, 0)),
                pl.BlockSpec((1, 1, group, width), lambda a, k, slabs: (slabs[k], a, 0, 0)),
            ],
            out_specs=pl.BlockSpec((group, width), lambda a, k, slabs: (a, k)),
        ),
        cost_estimate=pl.CostEstimate(
            flops=2 * groups * NS * group * group * width,
            bytes_accessed=4 * groups * NS * group * width,
            transcendentals=0,
        ),
    )(slab_index, maps[:, :, None], sources)


def window_kernel(core_ref, weight_ref, window_ref, aligned_ref, factor_ref, away_ref, keep_ref):
    width = factor_ref.shape[2]
    half = pl.num_programs(0) // 2
    y_window = jnp.dot(window_ref[0], aligned_ref[...], preferred_element_type=jnp.float32)
    y_window = y_window * weight_ref[0]
    columns, parts = [], []
    for k in range(NS):
        column = y_window[:, k * width : (k + 1) * width]
        for m in range(k):
            for part in parts[m]:
                column = column - jnp.dot(
                    part, factor_ref[pair_index(k, m)], preferred_element_type=jnp.float32
                )
        columns.append(column)
        parts.append(split(column))

    @pl.when(pl.program_id(0) < half)
    def _():
        for k in range(NS):
            away_ref[0, 0, :, k * width : (k + 1) * width] = columns[k]

    @pl.when(pl.program_id(0) >= half)
    def _():
        for k in range(NS):
            keep_ref[0, 0, :, k * width : (k + 1) * width] = columns[k]


def window_columns(place, scale, window_rows, aligned, factors, other, n_row, n_pole):
    share = window_rows.shape[1]
    side = n_pole // 4
    half = n_row * side
    depth, total = aligned.shape

    def window_at(i, place_ref):
        j = i % half
        core = jnp.where(i < half, 1 - place_ref[1], place_ref[1])
        second = 1 - place_ref[2] if other else place_ref[2]
        return (j // side) * n_pole + (j % side) * 4 + second * 2 + core, 0, 0

    def away_at(i, place_ref):
        j = jnp.minimum(i, half - 1)
        return j // side, j % side, 0, 0

    def keep_at(i, place_ref):
        j = jnp.maximum(i - half, 0)
        return j // side, j % side, 0, 0

    shape = jax.ShapeDtypeStruct((n_row, side, share, total), jnp.float32)
    return pl.pallas_call(
        window_kernel,
        out_shape=(shape, shape),
        grid_spec=pltpu.PrefetchScalarGridSpec(
            num_scalar_prefetch=1,
            grid=(2 * half,),
            in_specs=[
                pl.BlockSpec(memory_space=pltpu.SMEM),
                pl.BlockSpec((1, share, depth), window_at),
                pl.BlockSpec((depth, total), lambda i, c: (0, 0)),
                pl.BlockSpec(factors.shape, lambda i, c: (0, 0, 0)),
            ],
            out_specs=(
                pl.BlockSpec((1, 1, share, total), away_at),
                pl.BlockSpec((1, 1, share, total), keep_at),
            ),
        ),
        cost_estimate=pl.CostEstimate(
            flops=4 * half * share * depth * total,
            bytes_accessed=4 * half * share * (depth + 2 * total),
            transcendentals=0,
        ),
    )(place, scale, window_rows, aligned, factors)


def inner_kernel(place_ref, own_away_ref, own_keep_ref, away_ref, keep_ref, sum_ref):
    width = sum_ref.shape[1]

    @pl.when((pl.program_id(0) == 0) & (pl.program_id(1) == 0))
    def _():
        sum_ref[...] = jnp.zeros_like(sum_ref)

    for own_ref, term_ref in ((own_away_ref, away_ref), (own_keep_ref, keep_ref)):
        for m in range(NS):
            for part in split(term_ref[0, 0, :, m * width : (m + 1) * width]):
                for k in range(m, NS):
                    sum_ref[k * (k + 1) // 2 + m] += lax.dot_general(
                        own_ref[0, 0, :, k * width : (k + 1) * width],
                        part,
                        (((0,), (0,)), ((), ())),
                        preferred_element_type=jnp.float32,
                    )


def inner_products(place, own, away, keep, other, width):
    n_row, side, share, total = away.shape
    n_pole = 4 * side

    def own_at(flip):
        def at(d, j, place_ref):
            core = 1 - place_ref[1] if flip else place_ref[1]
            second = 1 - place_ref[2] if other else place_ref[2]
            return d, j * 4 + second * 2 + core, 0, 0

        return at

    def term_at(d, j, place_ref):
        return (place_ref[0] - d + n_row) % n_row, j, 0, 0

    pairs = NS * (NS + 1) // 2
    return pl.pallas_call(
        inner_kernel,
        out_shape=jax.ShapeDtypeStruct((pairs, width, width), jnp.float32),
        grid_spec=pltpu.PrefetchScalarGridSpec(
            num_scalar_prefetch=1,
            grid=(n_row, side),
            in_specs=[
                pl.BlockSpec((1, 1, share, total), own_at(True)),
                pl.BlockSpec((1, 1, share, total), own_at(False)),
                pl.BlockSpec((1, 1, share, total), term_at),
                pl.BlockSpec((1, 1, share, total), term_at),
            ],
            out_specs=pl.BlockSpec((pairs, width, width), lambda d, j, p: (0, 0, 0)),
        ),
        cost_estimate=pl.CostEstimate(
            flops=2 * n_row * n_pole * share * pairs * width * width,
            bytes_accessed=3 * n_row * n_pole * share * total,
            transcendentals=0,
        ),
    )(place, own, own, away, keep)


def staged(window, panels, row_map, panel_root, upper_blocks, diag_inverse, weights, pole_order):
    n_row, n_col, n_pole = (lax.axis_size(name) for name in ("row", "col", "pole"))
    row_index, col_index = lax.axis_index("row"), lax.axis_index("col")
    window_block = window[0]
    slab = panels[0, 0]
    width = slab.shape[1]
    group = window_block.shape[0] // n_row
    share = group // n_pole
    pole_weight = jnp.sum(jnp.where(jnp.arange(weights.shape[0]) == pole_order[0], weights, 0.0))
    pole_index = lax.axis_index("pole")
    core, second = pole_index % 2, (pole_index // 2) % 2
    place = jnp.stack([row_index, core, second]).astype(jnp.int32)
    slab_index = (col_index - panel_root[0] + n_col) % n_col
    local_map = row_map % group
    own_start = col_index * group

    slabs = [slab]
    for distance in range(1, n_col):
        slabs.append(shift(slab, "col", distance))
    own_map = lax.dynamic_slice_in_dim(local_map, own_start, group, 1)
    packed_map = jnp.concatenate([own_map // 32, own_map % 32]).astype(jnp.bfloat16).reshape(-1)
    packed_map = jnp.pad(packed_map, (0, -packed_map.shape[0] % width)).reshape(-1, width)
    part_rows = upper_blocks.shape[2]
    pairs = upper_blocks.shape[1]
    gathered = shift_gather(
        jnp.concatenate([upper_blocks[0].reshape(-1, width), packed_map]), "row"
    )
    own_slab = [shift_gather(lax.dynamic_slice_in_dim(slab, own_start, group, 0), "row")]
    factors = jnp.zeros((pairs, part_rows * n_row, width), upper_blocks.dtype)
    maps = []
    for back, g in enumerate(gathered):
        at = (row_index - back + n_row) % n_row
        factors = lax.dynamic_update_slice_in_dim(
            factors, g[: pairs * part_rows].reshape(pairs, part_rows, width), at * part_rows, 1
        )
        flat = g[pairs * part_rows :].reshape(-1)[: 2 * NS * group].astype(jnp.int32)
        maps.append((flat[: NS * group] * 32 + flat[NS * group :]).reshape(NS, group))

    stacked_slabs = jnp.stack(slabs).reshape(n_col, n_col, group, width)
    stacked_map = jnp.stack([local_map[:, c * group : (c + 1) * group] for c in range(n_col)])
    aligned = reorder(slab_index, stacked_map, stacked_slabs)
    own_slab += [
        shift_gather(lax.dynamic_slice_in_dim(other, own_start, group, 0), "row")
        for other in slabs[1:]
    ]

    window_rows = window_block.reshape(n_row * n_pole, share, window_block.shape[1])
    scale = (-pole_weight).reshape(1)
    first_away, first_keep = window_columns(
        place, scale, window_rows, aligned, factors, True, n_row, n_pole
    )
    last_away, last_keep = window_columns(
        place, scale, window_rows, aligned, factors, False, n_row, n_pole
    )
    first_come = swap(first_away, "pole", 1)
    last_come = swap(last_away, "pole", 1)
    step = share // CHUNKS if share % (8 * CHUNKS) == 0 else share
    pieces = [slice(at, at + step) for at in range(0, share, step)]
    sent = [first_keep[:, :, piece] + first_come[:, :, piece] for piece in pieces]
    kept = [last_keep[:, :, piece] + last_come[:, :, piece] for piece in pieces]
    _, own_slab = lax.optimization_barrier((sent, own_slab))
    column_parts = []
    for away, keep in zip(sent, kept):
        code, top = encode(away)
        code = swap(code, "pole", 2)
        top = swap(top, "pole", 2)
        total = keep + decode(code, top)
        column_parts.append(coded_sum(halving_sum(total, "pole", 4), "row"))
    summed_columns = jnp.stack(
        [
            jnp.concatenate([part[:, k * width : (k + 1) * width] for part in column_parts])
            for k in range(NS)
        ]
    )

    stacked_own = jnp.stack([jnp.stack(blocks) for blocks in own_slab])
    own = reorder(slab_index, jnp.stack(maps), stacked_own)
    own = own.reshape(n_row, n_pole, share, NS * width)
    products = inner_products(place, own, first_away, first_keep, True, width)
    products += inner_products(place, own, last_away, last_keep, False, width)
    inner = {(k, m): products[k * (k + 1) // 2 + m] for k in range(NS) for m in range(k + 1)}

    wide = [factors[e].astype(jnp.float32) for e in range(pairs)]
    spread = jnp.zeros((NS, diag_inverse.shape[2] * n_row, width), jnp.float32)
    spread = lax.dynamic_update_slice_in_dim(
        spread, diag_inverse[0] * (pole_weight / n_col), row_index * diag_inverse.shape[2], 1
    )
    diagonals, crossed = [], {}

    def inverse_block(m, n):
        if m == n:
            return diagonals[m]
        return crossed[m, n] if m < n else crossed[n, m].T

    for k in range(NS):
        diagonal = spread[k] - inner[k, k]
        for m in range(k):
            y_block = inner[k, m].T
            for n in range(k):
                y_block = y_block + precise(inverse_block(m, n), wide[pair_index(k, n)])
            crossed[m, k] = -y_block
            diagonal = diagonal + precise(wide[pair_index(k, m)].T, y_block)
        diagonals.append(diagonal)
    blocks = jnp.concatenate(diagonals, axis=1).reshape(n_row, n_pole, -1, NS * width)
    summed_diagonals = shift_sum(halving_sum(blocks, "pole", 1), "row")
    bit = 1
    while bit < n_col:
        summed_diagonals = summed_diagonals + lax.ppermute(
            summed_diagonals, "col", [(i, i ^ bit) for i in range(n_col)]
        )
        bit *= 2
    summed_diagonals = summed_diagonals.reshape(-1, NS, width).transpose(1, 0, 2)
    return (summed_columns[:, None], summed_diagonals)


def solution(mesh):
    return jax.shard_map(
        staged,
        mesh=mesh,
        in_specs=(
            P("pole", "col", "row"),
            P("pole", "col", "row", None),
            P(None, "row"),
            P("pole", None),
            P("pole", None, "row", None),
            P("pole", None, "row", None),
            P(),
            P("pole"),
        ),
        out_specs=(P(None, "col", ("row", "pole"), None), P(None, ("row", "pole"), None)),
        check_vma=False,
    )
```

profile of v0, /device:TPU:0, one launch (start us, length us, event | category | flops | bytes accessed | tf_op | source)
XLA Modules:
  0.0 301.1 jit_solution(300856751954513126)
XLA Ops:
  2.6 3.1 %collective-permute-start.1 = (bf16[216,256]{1,0:T(8,128)(2,1)S(1)}, bf16[216,256]{1,0:T(8,128)(2,1)S(1)}, u32[]{:S(2)}, u32[]{:S(2)}) collective-permute-start(bf16[216,256]{1,0:T(8,128)(2,1)S(1)} %pad_maximum_fusion.3), channel_id=1, source_target_pairs={{0,8},{8,16},{16,24},{24,0},{1,9},{9,17},{17,25},{25,1},{2,10},{10... | collective-permute-start | bytes 331784 | tf_op jit(solution)/shard_map/ppermute | solution.py:37
  5.6 2.6 collective-permute-start.2
  17.4 16.4 %collective-permute-done = bf16[2048,256]{1,0:T(8,128)(2,1)S(1)} collective-permute-done((bf16[2048,256]{1,0:T(8,128)(2,1)}, bf16[2048,256]{1,0:T(8,128)(2,1)S(1)}, u32[]{:S(2)}, u32[]{:S(2)}) %collective-permute-start) | collective-permute-done | bytes 1048608 | tf_op jit(solution)/shard_map/ppermute | solution.py:37
  35.5 8.3 %shard_map.95.aligned_ref = bf16[2048,768]{1,0:T(8,128)(2,1)} custom-call(s32[3]{0:T(128)} %and_select_fusion.slab_ref, s32[2,3,1,1024]{3,2,1,0:T(1,128)} %copy.23.map_ref, bf16[2,2,1024,256]{3,2,1,0:T(8,128)(2,1)} %pad_maximum_fusion.1.rows_ref), custom_call_target="tpu_custom_call" | custom-call | flops 3221225472 | bytes 6291456 | tf_op jit(solution)/shard_map/pallas_call | solution.py:104
  43.8 15.0 %shard_map.97 = (f32[4,1,256,768]{3,2,1,0:T(8,128)}, f32[4,1,256,768]{3,2,1,0:T(8,128)}) custom-call(s32[3]{0:T(128)} %pad_add_fusion.core_ref.place_ref, f32[1]{0:T(128)} %bitcast.4.weight_ref, bf16[16,256,2048]{2,1,0:T(8,128)(2,1)} %bitcast.195, bf16[2048,768]{1,0:T(8,128)(2,1)} %shard_map.95.aligned_ref, bf16[3,256,256]{2,1,0:T(8,128)(2,1)} %copy-done.5), custom_call_target="tpu_custom_call" | custom-call | flops 6442450944 | bytes 14680064 | tf_op jit(solution)/shard_map/pallas_call | solution.py:172
  58.9 1.9 dynamic-slice_bitcast_fusion
  61.8 2.8 collective-permute-start.24
  69.2 1.9 constant_dynamic-slice_fusion.1
  71.7 6.2 %collective-permute-done.22 = bf16[1024,256]{1,0:T(8,128)(2,1)} collective-permute-done((bf16[1024,256]{1,0:T(8,128)(2,1)}, bf16[1024,256]{1,0:T(8,128)(2,1)}, u32[]{:S(2)}, u32[]{:S(2)}) %collective-permute-start.22) | collective-permute-done | bytes 524320 | tf_op jit(solution)/shard_map/ppermute | solution.py:37
  80.6 15.2 %shard_map.96 = (f32[4,1,256,768]{3,2,1,0:T(8,128)}, f32[4,1,256,768]{3,2,1,0:T(8,128)}) custom-call(s32[3]{0:T(128)} %pad_add_fusion.core_ref.place_ref, f32[1]{0:T(128)} %bitcast.4.weight_ref, bf16[16,256,2048]{2,1,0:T(8,128)(2,1)} %bitcast.196, bf16[2048,768]{1,0:T(8,128)(2,1)} %shard_map.95.aligned_ref, bf16[3,256,256]{2,1,0:T(8,128)(2,1)} %copy-done.5), custom_call_target="tpu_custom_call" | custom-call | flops 6442450944 | bytes 14680064 | tf_op jit(solution)/shard_map/pallas_call | solution.py:172
  95.9 3.9 %abs_reduce_fusion.1 = (f32[4,128]{1,0:T(4,128)S(1)}, f32[4,1,128,768]{3,2,1,0:T(8,128)}, f32[4,128]{1,0:T(4,128)S(1)}, f32[4,1,128,768]{3,2,1,0:T(8,128)}) fusion(f32[4,1,256,768]{3,2,1,0:T(8,128)} %copy-done.7, f32[4,1,256,768]{3,2,1,0:T(8,128)S(1)} %copy-done.1), kind=kLoop, calls=%fused_computation.23 | loop fusion | flops 2358272 | bytes 9441280 | tf_op jit(solution)/shard_map/reduce_max | solution.py:41
  100.4 11.2 %collective-permute-done.25 = bf16[1024,256]{1,0:T(8,128)(2,1)} collective-permute-done((bf16[1024,256]{1,0:T(8,128)(2,1)}, bf16[1024,256]{1,0:T(8,128)(2,1)}, u32[]{:S(2)}, u32[]{:S(2)}) %collective-permute-start.25) | collective-permute-done | bytes 524320 | tf_op jit(solution)/shard_map/ppermute | solution.py:37
  111.6 33.2 %collective-permute-done.26 = bf16[1024,256]{1,0:T(8,128)(2,1)} collective-permute-done((bf16[1024,256]{1,0:T(8,128)(2,1)}, bf16[1024,256]{1,0:T(8,128)(2,1)}, u32[]{:S(2)}, u32[]{:S(2)}) %collective-permute-start.26) | collective-permute-done | bytes 524320 | tf_op jit(solution)/shard_map/ppermute | solution.py:37
  144.8 2.4 maximum_bitcast_fusion
  147.2 2.4 pad_maximum_fusion.rows_ref
  149.7 14.6 %shard_map.98 = bf16[4096,768]{1,0:T(8,128)(2,1)} custom-call(s32[3]{0:T(128)} %and_select_fusion.slab_ref, s32[4,3,1,1024]{3,2,1,0:T(1,128)} %copy.25.map_ref, bf16[2,4,1024,256]{3,2,1,0:T(8,128)(2,1)} %pad_maximum_fusion.rows_ref), custom_call_target="tpu_custom_call" | custom-call | flops 6442450944 | bytes 12582912 | tf_op jit(solution)/shard_map/pallas_call | solution.py:104
  164.2 8.5 %shard_map.99 = f32[6,256,256]{2,1,0:T(8,128)} custom-call(s32[3]{0:T(128)} %pad_add_fusion.core_ref.place_ref, bf16[4,4,256,768]{3,2,1,0:T(8,128)(2,1)} %bitcast.181, bf16[4,4,256,768]{3,2,1,0:T(8,128)(2,1)} %bitcast.182, f32[4,1,256,768]{3,2,1,0:T(8,128)} %get-tuple-element.17.away_ref, f32[4,1,256,768]{3,2,1,0:T(8,128)} %get-tuple-element.16.keep_ref), custom_call_target="tpu_custom_call" | custom-call | flops 3221225472 | bytes 9437184 | tf_op jit(solution)/shard_map/pallas_call | solution.py:232
  172.7 8.7 %shard_map.100 = f32[6,256,256]{2,1,0:T(8,128)} custom-call(s32[3]{0:T(128)} %pad_add_fusion.core_ref.place_ref, bf16[4,4,256,768]{3,2,1,0:T(8,128)(2,1)} %bitcast.183, bf16[4,4,256,768]{3,2,1,0:T(8,128)(2,1)} %bitcast.184, f32[4,1,256,768]{3,2,1,0:T(8,128)} %get-tuple-element.15.away_ref, f32[4,1,256,768]{3,2,1,0:T(8,128)} %get-tuple-element.14.keep_ref), custom_call_target="tpu_custom_call" | custom-call | flops 3221225472 | bytes 9437184 | tf_op jit(solution)/shard_map/pallas_call | solution.py:232
  195.8 19.9 %collective-permute-done.29 = f32[4,1,16,768]{3,2,1,0:T(8,128)S(1)} collective-permute-done((f32[4,1,16,768]{3,2,1,0:T(8,128)S(1)}, f32[4,1,16,768]{3,2,1,0:T(8,128)S(1)}, u32[]{:S(2)}, u32[]{:S(2)}) %collective-permute-start.29) | collective-permute-done | bytes 196640 | tf_op jit(solution)/shard_map/ppermute | solution.py:32
  215.8 10.7 %collective-permute-start.32 = (f32[16,768]{1,0:T(8,128)S(1)}, f32[16,768]{1,0:T(8,128)S(1)}, u32[]{:S(2)}, u32[]{:S(2)}) collective-permute-start(f32[16,768]{1,0:T(8,128)S(1)} %get-tuple-element.59), channel_id=1, source_target_pairs={{0,24},{8,0},{16,8},{24,16},{1,25},{9,1},{17,9},{25,17},{2,26},{10... | collective-permute-start | bytes 147464 | tf_op jit(solution)/shard_map/ppermute | solution.py:37
  228.0 3.4 %collective-permute-done.7 = f32[4,1,128]{2,0,1:T(4,128)S(1)} collective-permute-done((f32[4,1,128]{2,0,1:T(4,128)S(1)}, f32[4,1,128]{2,0,1:T(4,128)S(1)}, u32[]{:S(2)}, u32[]{:S(2)}) %collective-permute-start.7) | collective-permute-done | bytes 2080 | tf_op jit(solution)/shard_map/ppermute | solution.py:32
  231.4 10.2 %collective-permute-start.31 = (f32[16,768]{1,0:T(8,128)S(1)}, f32[16,768]{1,0:T(8,128)S(1)}, u32[]{:S(2)}, u32[]{:S(2)}) collective-permute-start(f32[16,768]{1,0:T(8,128)S(1)} %get-tuple-element.60), channel_id=1, source_target_pairs={{0,16},{8,24},{16,0},{24,8},{1,17},{9,25},{17,1},{25,9},{2,18},{10... | collective-permute-start | bytes 147464 | tf_op jit(solution)/shard_map/ppermute | solution.py:37
  245.1 2.4 collective-permute-done.30
  249.1 2.6 collective-permute-done.33
  252.4 3.4 %fusion.5 = (f32[4,128]{1,0:T(4,128)S(1)}, f32[4,1,128,768]{3,2,1,0:T(8,128)S(1)}, f32[4,128]{1,0:T(4,128)S(1)}, f32[4,1,128,768]{3,2,1,0:T(8,128)S(1)}) fusion(f32[4,128]{1,0:T(4,128)S(1)} %multiply_bitcast_fusion.1, s16[4,1,128,768]{3,2,1,0:T(8,128)(2,1)} %collective-permute-done.6, f32[4,1,256,768]{3,2,1,0:T(8,128)} %collective-permute-done.4, ...), kind=kLoop, calls=%fused_computation.17 | loop fusion | flops 4717568 | bytes 11018240 | tf_op jit(solution)/shard_map/reduce_max | solution.py:41
  259.5 3.9 %collective-permute-start.21 = (f32[128]{0:T(128)S(1)}, f32[128]{0:T(128)S(1)}, u32[]{:S(2)}, u32[]{:S(2)}) collective-permute-start(f32[128]{0:T(128)S(1)} %get-tuple-element.73), channel_id=1, source_target_pairs={{0,24},{8,0},{16,8},{24,16},{1,25},{9,1},{17,9},{25,17},{2,26},{10... | collective-permute-start | bytes 1544 | tf_op jit(solution)/shard_map/ppermute | solution.py:37
  263.4 3.9 %collective-permute-done.21 = f32[128]{0:T(128)S(1)} collective-permute-done((f32[128]{0:T(128)S(1)}, f32[128]{0:T(128)S(1)}, u32[]{:S(2)}, u32[]{:S(2)}) %collective-permute-start.21) | collective-permute-done | bytes 544 | tf_op jit(solution)/shard_map/ppermute | solution.py:37
  267.4 6.4 %collective-permute-start.17 = (f32[128]{0:T(128)S(1)}, f32[128]{0:T(128)S(1)}, u32[]{:S(2)}, u32[]{:S(2)}) collective-permute-start(f32[128]{0:T(128)S(1)} %get-tuple-element.71), channel_id=1, source_target_pairs={{0,8},{8,16},{16,24},{24,0},{1,9},{9,17},{17,25},{25,1},{2,10},{10... | collective-permute-start | bytes 1544 | tf_op jit(solution)/shard_map/ppermute | solution.py:37
  275.9 3.6 %collective-permute-done.13 = f32[128]{0:T(128)S(1)} collective-permute-done((f32[128]{0:T(128)S(1)}, f32[128]{0:T(128)S(1)}, u32[]{:S(2)}, u32[]{:S(2)}) %collective-permute-start.13) | collective-permute-done | bytes 544 | tf_op jit(solution)/shard_map/ppermute | solution.py:37
  280.3 3.7 %collective-permute-done.11 = f32[128]{0:T(128)S(1)} collective-permute-done((f32[128]{0:T(128)S(1)}, f32[128]{0:T(128)S(1)}, u32[]{:S(2)}, u32[]{:S(2)}) %collective-permute-start.11) | collective-permute-done | bytes 544 | tf_op jit(solution)/shard_map/ppermute | solution.py:37
  285.3 4.1 %collective-permute-done.9 = f32[128]{0:T(128)S(1)} collective-permute-done((f32[128]{0:T(128)S(1)}, f32[128]{0:T(128)S(1)}, u32[]{:S(2)}, u32[]{:S(2)}) %collective-permute-start.9) | collective-permute-done | bytes 544 | tf_op jit(solution)/shard_map/ppermute | solution.py:37
  291.6 8.2 %collective-permute-done.10 = s16[128,768]{1,0:T(8,128)(2,1)S(1)} collective-permute-done((s16[128,768]{1,0:T(8,128)(2,1)S(1)}, s16[128,768]{1,0:T(8,128)(2,1)S(1)}, u32[]{:S(2)}, u32[]{:S(2)}) %collective-permute-start.10) | collective-permute-done | bytes 196640 | tf_op jit(solution)/shard_map/ppermute | solution.py:37
  (155 shorter events, 53.3 us)
Async XLA Ops:
  2.6 14.7 %collective-permute-start.1 = (bf16[216,256]{1,0:T(8,128)(2,1)S(1)}, bf16[216,256]{1,0:T(8,128)(2,1)S(1)}, u32[]{:S(2)}, u32[]{:S(2)}) collective-permute-start(bf16[216,256]{1,0:T(8,128)(2,1)S(1)} %pad_maximum_fusion.3), channel_id=1, source_target_pairs={{0,8},{8,16},{16,24},{24,0},{1,9},{9,17},{17,25},{25,1},{2,10},{10... | collective-permute-start | bytes 331784 | tf_op jit(solution)/shard_map/ppermute | solution.py:37
  5.6 11.6 %collective-permute-start.2 = (bf16[216,256]{1,0:T(8,128)(2,1)S(1)}, bf16[216,256]{1,0:T(8,128)(2,1)S(1)}, u32[]{:S(2)}, u32[]{:S(2)}) collective-permute-start(bf16[216,256]{1,0:T(8,128)(2,1)S(1)} %pad_maximum_fusion.3), channel_id=1, source_target_pairs={{0,16},{8,24},{16,0},{24,8},{1,17},{9,25},{17,1},{25,9},{2,18},{10... | collective-permute-start | bytes 331784 | tf_op jit(solution)/shard_map/ppermute | solution.py:37
  8.2 9.1 %collective-permute-start.3 = (bf16[216,256]{1,0:T(8,128)(2,1)S(1)}, bf16[216,256]{1,0:T(8,128)(2,1)S(1)}, u32[]{:S(2)}, u32[]{:S(2)}) collective-permute-start(bf16[216,256]{1,0:T(8,128)(2,1)S(1)} %pad_maximum_fusion.3), channel_id=1, source_target_pairs={{0,24},{8,0},{16,8},{24,16},{1,25},{9,1},{17,9},{25,17},{2,26},{10... | collective-permute-start | bytes 331784 | tf_op jit(solution)/shard_map/ppermute | solution.py:37
  9.5 24.3 %collective-permute-start = (bf16[2048,256]{1,0:T(8,128)(2,1)}, bf16[2048,256]{1,0:T(8,128)(2,1)S(1)}, u32[]{:S(2)}, u32[]{:S(2)}) collective-permute-start(bf16[2048,256]{1,0:T(8,128)(2,1)} %bitcast.187), channel_id=1, source_target_pairs={{0,4},{4,0},{1,5},{5,1},{2,6},{6,2},{3,7},{7,3},{8,12},{12,8},{9,1... | collective-permute-start | bytes 3145736 | tf_op jit(solution)/shard_map/ppermute | solution.py:37
  58.9 19.0 %collective-permute-start.5 = (f32[4,1,256,768]{3,2,1,0:T(8,128)}, f32[4,1,256,768]{3,2,1,0:T(8,128)S(1)}, u32[]{:S(2)}, u32[]{:S(2)}) collective-permute-start(f32[4,1,256,768]{3,2,1,0:T(8,128)} %get-tuple-element.17.away_ref), channel_id=1, source_target_pairs={{0,1},{1,0},{2,3},{3,2},{4,5},{5,4},{6,7},{7,6},{8,9},{9,8},{10,11... | collective-permute-start | bytes 9437192 | tf_op jit(solution)/shard_map/ppermute | solution.py:32
  60.8 17.1 %collective-permute-start.22 = (bf16[1024,256]{1,0:T(8,128)(2,1)}, bf16[1024,256]{1,0:T(8,128)(2,1)}, u32[]{:S(2)}, u32[]{:S(2)}) collective-permute-start(bf16[1024,256]{1,0:T(8,128)(2,1)} %dynamic-slice_bitcast_fusion), channel_id=1, source_target_pairs={{0,8},{8,16},{16,24},{24,0},{1,9},{9,17},{17,25},{25,1},{2,10},{10... | collective-permute-start | bytes 1572872 | tf_op jit(solution)/shard_map/ppermute | solution.py:37
  61.5 38.9 %collective-permute-start.23 = (bf16[1024,256]{1,0:T(8,128)(2,1)}, bf16[1024,256]{1,0:T(8,128)(2,1)}, u32[]{:S(2)}, u32[]{:S(2)}) collective-permute-start(bf16[1024,256]{1,0:T(8,128)(2,1)} %dynamic-slice_bitcast_fusion), channel_id=1, source_target_pairs={{0,16},{8,24},{16,0},{24,8},{1,17},{9,25},{17,1},{25,9},{2,18},{10... | collective-permute-start | bytes 1572872 | tf_op jit(solution)/shard_map/ppermute | solution.py:37
  61.8 38.6 %collective-permute-start.24 = (bf16[1024,256]{1,0:T(8,128)(2,1)}, bf16[1024,256]{1,0:T(8,128)(2,1)}, u32[]{:S(2)}, u32[]{:S(2)}) collective-permute-start(bf16[1024,256]{1,0:T(8,128)(2,1)} %dynamic-slice_bitcast_fusion), channel_id=1, source_target_pairs={{0,24},{8,0},{16,8},{24,16},{1,25},{9,1},{17,9},{25,17},{2,26},{10... | collective-permute-start | bytes 1572872 | tf_op jit(solution)/shard_map/ppermute | solution.py:37
  71.1 40.5 %collective-permute-start.25 = (bf16[1024,256]{1,0:T(8,128)(2,1)}, bf16[1024,256]{1,0:T(8,128)(2,1)}, u32[]{:S(2)}, u32[]{:S(2)}) collective-permute-start(bf16[1024,256]{1,0:T(8,128)(2,1)} %constant_dynamic-slice_fusion.1), channel_id=1, source_target_pairs={{0,8},{8,16},{16,24},{24,0},{1,9},{9,17},{17,25},{25,1},{2,10},{10... | collective-permute-start | bytes 1572872 | tf_op jit(solution)/shard_map/ppermute | solution.py:37
  77.9 66.9 %collective-permute-start.26 = (bf16[1024,256]{1,0:T(8,128)(2,1)}, bf16[1024,256]{1,0:T(8,128)(2,1)}, u32[]{:S(2)}, u32[]{:S(2)}) collective-permute-start(bf16[1024,256]{1,0:T(8,128)(2,1)} %constant_dynamic-slice_fusion.1), channel_id=1, source_target_pairs={{0,16},{8,24},{16,0},{24,8},{1,17},{9,25},{17,1},{25,9},{2,18},{10... | collective-permute-start | bytes 1572872 | tf_op jit(solution)/shard_map/ppermute | solution.py:37
  79.5 65.3 %collective-permute-start.27 = (bf16[1024,256]{1,0:T(8,128)(2,1)}, bf16[1024,256]{1,0:T(8,128)(2,1)}, u32[]{:S(2)}, u32[]{:S(2)}) collective-permute-start(bf16[1024,256]{1,0:T(8,128)(2,1)} %constant_dynamic-slice_fusion.1), channel_id=1, source_target_pairs={{0,24},{8,0},{16,8},{24,16},{1,25},{9,1},{17,9},{25,17},{2,26},{10... | collective-permute-start | bytes 1572872 | tf_op jit(solution)/shard_map/ppermute | solution.py:37
  100.4 152.0 %collective-permute-start.4 = (f32[4,1,256,768]{3,2,1,0:T(8,128)}, f32[4,1,256,768]{3,2,1,0:T(8,128)}, u32[]{:S(2)}, u32[]{:S(2)}) collective-permute-start(f32[4,1,256,768]{3,2,1,0:T(8,128)} %get-tuple-element.15.away_ref), channel_id=1, source_target_pairs={{0,1},{1,0},{2,3},{3,2},{4,5},{5,4},{6,7},{7,6},{8,9},{9,8},{10,11... | collective-permute-start | bytes 9437192 | tf_op jit(solution)/shard_map/ppermute | solution.py:32
  190.9 61.5 %collective-permute-start.6 = (s16[4,1,128,768]{3,2,1,0:T(8,128)(2,1)}, s16[4,1,128,768]{3,2,1,0:T(8,128)(2,1)}, u32[]{:S(2)}, u32[]{:S(2)}) collective-permute-start(s16[4,1,128,768]{3,2,1,0:T(8,128)(2,1)} %round-nearest-even_convert_fusion.1), channel_id=1, source_target_pairs={{0,2},{1,3},{2,0},{3,1},{4,6},{5,7},{6,4},{7,5},{8,10},{9,11},{10,... | collective-permute-start | bytes 2359304 | tf_op jit(solution)/shard_map/ppermute | solution.py:32
  192.5 23.2 %collective-permute-start.29 = (f32[4,1,16,768]{3,2,1,0:T(8,128)S(1)}, f32[4,1,16,768]{3,2,1,0:T(8,128)S(1)}, u32[]{:S(2)}, u32[]{:S(2)}) collective-permute-start(f32[4,1,16,768]{3,2,1,0:T(8,128)S(1)} %constant_dynamic-slice_fusion), channel_id=1, source_target_pairs={{0,2},{1,3},{2,0},{3,1},{4,6},{5,7},{6,4},{7,5},{8,10},{9,11},{10,... | collective-permute-start | bytes 589832 | tf_op jit(solution)/shard_map/ppermute | solution.py:32
  194.3 58.1 %collective-permute-start.14 = (s16[4,1,128,768]{3,2,1,0:T(8,128)(2,1)}, s16[4,1,128,768]{3,2,1,0:T(8,128)(2,1)}, u32[]{:S(2)}, u32[]{:S(2)}) collective-permute-start(s16[4,1,128,768]{3,2,1,0:T(8,128)(2,1)} %round-nearest-even_convert_fusion), channel_id=1, source_target_pairs={{0,2},{1,3},{2,0},{3,1},{4,6},{5,7},{6,4},{7,5},{8,10},{9,11},{10,... | collective-permute-start | bytes 2359304 | tf_op jit(solution)/shard_map/ppermute | solution.py:32
  215.8 25.8 %collective-permute-start.32 = (f32[16,768]{1,0:T(8,128)S(1)}, f32[16,768]{1,0:T(8,128)S(1)}, u32[]{:S(2)}, u32[]{:S(2)}) collective-permute-start(f32[16,768]{1,0:T(8,128)S(1)} %get-tuple-element.59), channel_id=1, source_target_pairs={{0,24},{8,0},{16,8},{24,16},{1,25},{9,1},{17,9},{25,17},{2,26},{10... | collective-permute-start | bytes 147464 | tf_op jit(solution)/shard_map/ppermute | solution.py:37
  226.5 4.9 %collective-permute-start.7 = (f32[4,1,128]{2,0,1:T(4,128)S(1)}, f32[4,1,128]{2,0,1:T(4,128)S(1)}, u32[]{:S(2)}, u32[]{:S(2)}) collective-permute-start(f32[4,1,128]{2,0,1:T(4,128)S(1)} %get-tuple-element.70), channel_id=1, source_target_pairs={{0,2},{1,3},{2,0},{3,1},{4,6},{5,7},{6,4},{7,5},{8,10},{9,11},{10,... | collective-permute-start | bytes 6152 | tf_op jit(solution)/shard_map/ppermute | solution.py:32
  231.4 12.2 %collective-permute-start.31 = (f32[16,768]{1,0:T(8,128)S(1)}, f32[16,768]{1,0:T(8,128)S(1)}, u32[]{:S(2)}, u32[]{:S(2)}) collective-permute-start(f32[16,768]{1,0:T(8,128)S(1)} %get-tuple-element.60), channel_id=1, source_target_pairs={{0,16},{8,24},{16,0},{24,8},{1,17},{9,25},{17,1},{25,9},{2,18},{10... | collective-permute-start | bytes 147464 | tf_op jit(solution)/shard_map/ppermute | solution.py:37
  241.6 6.0 %collective-permute-start.30 = (f32[16,768]{1,0:T(8,128)S(1)}, f32[16,768]{1,0:T(8,128)S(1)}, u32[]{:S(2)}, u32[]{:S(2)}) collective-permute-start(f32[16,768]{1,0:T(8,128)S(1)} %get-tuple-element.58), channel_id=1, source_target_pairs={{0,8},{8,16},{16,24},{24,0},{1,9},{9,17},{17,25},{25,1},{2,10},{10... | collective-permute-start | bytes 147464 | tf_op jit(solution)/shard_map/ppermute | solution.py:37
  243.6 5.5 %collective-permute-start.15 = (f32[4,1,128]{2,0,1:T(4,128)S(1)}, f32[4,1,128]{2,0,1:T(4,128)S(1)}, u32[]{:S(2)}, u32[]{:S(2)}) collective-permute-start(f32[4,1,128]{2,0,1:T(4,128)S(1)} %get-tuple-element.77), channel_id=1, source_target_pairs={{0,2},{1,3},{2,0},{3,1},{4,6},{5,7},{6,4},{7,5},{8,10},{9,11},{10,... | collective-permute-start | bytes 6152 | tf_op jit(solution)/shard_map/ppermute | solution.py:32
  256.4 33.0 %collective-permute-start.20 = (s16[128,768]{1,0:T(8,128)(2,1)S(1)}, s16[128,768]{1,0:T(8,128)(2,1)S(1)}, u32[]{:S(2)}, u32[]{:S(2)}) collective-permute-start(s16[128,768]{1,0:T(8,128)(2,1)S(1)} %get-tuple-element.50), channel_id=1, source_target_pairs={{0,24},{8,0},{16,8},{24,16},{1,25},{9,1},{17,9},{25,17},{2,26},{10... | collective-permute-start | bytes 589832 | tf_op jit(solution)/shard_map/ppermute | solution.py:37
  258.0 33.3 %collective-permute-start.18 = (s16[128,768]{1,0:T(8,128)(2,1)S(1)}, s16[128,768]{1,0:T(8,128)(2,1)S(1)}, u32[]{:S(2)}, u32[]{:S(2)}) collective-permute-start(s16[128,768]{1,0:T(8,128)(2,1)S(1)} %get-tuple-element.51), channel_id=1, source_target_pairs={{0,16},{8,24},{16,0},{24,8},{1,17},{9,25},{17,1},{25,9},{2,18},{10... | collective-permute-start | bytes 589832 | tf_op jit(solution)/shard_map/ppermute | solution.py:37
  259.5 31.8 %collective-permute-start.16 = (s16[128,768]{1,0:T(8,128)(2,1)S(1)}, s16[128,768]{1,0:T(8,128)(2,1)S(1)}, u32[]{:S(2)}, u32[]{:S(2)}) collective-permute-start(s16[128,768]{1,0:T(8,128)(2,1)S(1)} %get-tuple-element.49), channel_id=1, source_target_pairs={{0,8},{8,16},{16,24},{24,0},{1,9},{9,17},{17,25},{25,1},{2,10},{10... | collective-permute-start | bytes 589832 | tf_op jit(solution)/shard_map/ppermute | solution.py:37
  259.5 7.9 %collective-permute-start.21 = (f32[128]{0:T(128)S(1)}, f32[128]{0:T(128)S(1)}, u32[]{:S(2)}, u32[]{:S(2)}) collective-permute-start(f32[128]{0:T(128)S(1)} %get-tuple-element.73), channel_id=1, source_target_pairs={{0,24},{8,0},{16,8},{24,16},{1,25},{9,1},{17,9},{25,17},{2,26},{10... | collective-permute-start | bytes 1544 | tf_op jit(solution)/shard_map/ppermute | solution.py:37
  263.4 10.4 %collective-permute-start.19 = (f32[128]{0:T(128)S(1)}, f32[128]{0:T(128)S(1)}, u32[]{:S(2)}, u32[]{:S(2)}) collective-permute-start(f32[128]{0:T(128)S(1)} %get-tuple-element.72), channel_id=1, source_target_pairs={{0,16},{8,24},{16,0},{24,8},{1,17},{9,25},{17,1},{25,9},{2,18},{10... | collective-permute-start | bytes 1544 | tf_op jit(solution)/shard_map/ppermute | solution.py:37
  267.4 7.7 %collective-permute-start.17 = (f32[128]{0:T(128)S(1)}, f32[128]{0:T(128)S(1)}, u32[]{:S(2)}, u32[]{:S(2)}) collective-permute-start(f32[128]{0:T(128)S(1)} %get-tuple-element.71), channel_id=1, source_target_pairs={{0,8},{8,16},{16,24},{24,0},{1,9},{9,17},{17,25},{25,1},{2,10},{10... | collective-permute-start | bytes 1544 | tf_op jit(solution)/shard_map/ppermute | solution.py:37
  273.7 17.8 %collective-permute-start.12 = (s16[128,768]{1,0:T(8,128)(2,1)S(1)}, s16[128,768]{1,0:T(8,128)(2,1)S(1)}, u32[]{:S(2)}, u32[]{:S(2)}) collective-permute-start(s16[128,768]{1,0:T(8,128)(2,1)S(1)} %get-tuple-element.47), channel_id=1, source_target_pairs={{0,24},{8,0},{16,8},{24,16},{1,25},{9,1},{17,9},{25,17},{2,26},{10... | collective-permute-start | bytes 589832 | tf_op jit(solution)/shard_map/ppermute | solution.py:37
  275.0 4.5 %collective-permute-start.13 = (f32[128]{0:T(128)S(1)}, f32[128]{0:T(128)S(1)}, u32[]{:S(2)}, u32[]{:S(2)}) collective-permute-start(f32[128]{0:T(128)S(1)} %get-tuple-element.66), channel_id=1, source_target_pairs={{0,24},{8,0},{16,8},{24,16},{1,25},{9,1},{17,9},{25,17},{2,26},{10... | collective-permute-start | bytes 1544 | tf_op jit(solution)/shard_map/ppermute | solution.py:37
  279.5 4.5 %collective-permute-start.11 = (f32[128]{0:T(128)S(1)}, f32[128]{0:T(128)S(1)}, u32[]{:S(2)}, u32[]{:S(2)}) collective-permute-start(f32[128]{0:T(128)S(1)} %get-tuple-element.65), channel_id=1, source_target_pairs={{0,16},{8,24},{16,0},{24,8},{1,17},{9,25},{17,1},{25,9},{2,18},{10... | collective-permute-start | bytes 1544 | tf_op jit(solution)/shard_map/ppermute | solution.py:37
  284.0 5.5 %collective-permute-start.9 = (f32[128]{0:T(128)S(1)}, f32[128]{0:T(128)S(1)}, u32[]{:S(2)}, u32[]{:S(2)}) collective-permute-start(f32[128]{0:T(128)S(1)} %get-tuple-element.64), channel_id=1, source_target_pairs={{0,8},{8,16},{16,24},{24,0},{1,9},{9,17},{17,25},{25,1},{2,10},{10... | collective-permute-start | bytes 1544 | tf_op jit(solution)/shard_map/ppermute | solution.py:37
  289.4 10.4 %collective-permute-start.10 = (s16[128,768]{1,0:T(8,128)(2,1)S(1)}, s16[128,768]{1,0:T(8,128)(2,1)S(1)}, u32[]{:S(2)}, u32[]{:S(2)}) collective-permute-start(s16[128,768]{1,0:T(8,128)(2,1)S(1)} %get-tuple-element.48), channel_id=1, source_target_pairs={{0,16},{8,24},{16,0},{24,8},{1,17},{9,25},{17,1},{25,9},{2,18},{10... | collective-permute-start | bytes 589832 | tf_op jit(solution)/shard_map/ppermute | solution.py:37
  289.4 10.4 %collective-permute-start.8 = (s16[128,768]{1,0:T(8,128)(2,1)S(1)}, s16[128,768]{1,0:T(8,128)(2,1)S(1)}, u32[]{:S(2)}, u32[]{:S(2)}) collective-permute-start(s16[128,768]{1,0:T(8,128)(2,1)S(1)} %get-tuple-element.46), channel_id=1, source_target_pairs={{0,8},{8,16},{16,24},{24,0},{1,9},{9,17},{17,25},{25,1},{2,10},{10... | collective-permute-start | bytes 589832 | tf_op jit(solution)/shard_map/ppermute | solution.py:37
  (15 other events, 197.2 us)
where the time goes:
time: 303 us; the launch traced here: 301 us
  waiting for transfers between devices  121 us (40%)
  Pallas kernels  70.3 us (23%)
  starting transfers between devices  63.6 us (21%)
  other arithmetic  28.4 us (9%)
  local copies, waits for them, and re-layouts  10.6 us (3%)
  matrix products  4.51 us (1%)
  between operations  3.2 us (1%)
    ppermute x25, waiting for transfers between devices, shift(): lax.ppermute(block, axis_name, [(i, (i + distance) % size) for i in range...  94.6 us
    ppermute x25, starting transfers between devices, shift(): lax.ppermute(block, axis_name, [(i, (i + distance) % size) for i in range...  55.3 us
    pallas_call x2, Pallas kernels, window_columns(): pl.pallas_call(window_kernel, out_shape=(shape, shape), grid_spec=pltpu.P...  30.3 us
    ppermute x8, waiting for transfers between devices, swap(): return lax.ppermute(block, axis_name, [(i, i ^ bit) for i in range(size)])  23.3 us
    pallas_call x2, Pallas kernels, reorder(): pl.pallas_call(reorder_kernel, out_shape=jax.ShapeDtypeStruct((groups * g...  22.9 us
    pallas_call x2, Pallas kernels, inner_products(): pl.pallas_call(inner_kernel, out_shape=jax.ShapeDtypeStruct((pairs, width...  17.2 us
    reduce_max x2, other arithmetic, encode(): top = jnp.maximum(jnp.max(jnp.abs(value), axis=-1), 1e-30)  7.3 us
    ppermute x8, starting transfers between devices, swap(): return lax.ppermute(block, axis_name, [(i, i ^ bit) for i in range(size)])  6.73 us
  transfers between devices with their start and end apart: 34, of which 15 were waited for; matrix products, arithmetic and copies ran while one was open for 11% of the time, Pallas kernels for 16%

commit v1 on v0

--- a/solution.py
+++ b/solution.py
@@ -366,8 +366,462 @@
     return (summed_columns[:, None], summed_diagonals)
 
 
+MESH = pl.DeviceIdType.MESH
+LEVELS = 32000.0
+
+
+def code_of(value):
+    top = jnp.maximum(jnp.max(jnp.abs(value), axis=0, keepdims=True), 1e-30)
+    return jnp.round(value * (LEVELS / top)).astype(jnp.int32).astype(jnp.int16), top
+
+
+def value_of(code, top):
+    return code.astype(jnp.int32).astype(jnp.float32) * (top * (1.0 / LEVELS))
+
+
+def fused_kernel(
+    weights_ref, order_ref, root_ref, window_ref, slab_ref, map_ref, upper_ref, diag_ref,
+    columns_ref, diagonal_ref,
+    win, own_slab, far_slab, maps, fac, al, y, core_in, y_out, y_out_top, y_in, y_in_top,
+    z_out, z_out_top, z_in, z_in_top, inner, spread, g_all, g_core, g_half, g_y, g_sum, g_z, g_x, g_last,
+    x_send, x_recv, here, win_sem, own_send, own_recv, small_send, small_recv,
+    core_send, core_recv, y_send, y_recv, z_send, z_recv,
+    gc_send, gc_recv, gy_send, gy_recv, gz_send, gz_recv, gx_send, gx_recv,
+):
+    n_row, n_col, n_pole = (lax.axis_size(name) for name in ("row", "col", "pole"))
+    r, c, p = (lax.axis_index(name) for name in ("row", "col", "pole"))
+    side, core = p // 2, p % 2
+    share, width = columns_ref.shape[1:]
+    group = share * n_pole
+    depth = diagonal_ref.shape[1]
+    part = upper_ref.shape[1]
+    to_col, to_core, to_side = {"col": 1 - c}, {"pole": side * 2 + 1 - core}, {"pole": (1 - side) * 2 + core}
+
+    def remote(src, dst, send, recv, device):
+        return pltpu.make_async_remote_copy(
+            src_ref=src, dst_ref=dst, send_sem=send, recv_sem=recv, device_id=device, device_id_type=MESH
+        )
+
+    def half(at):
+        return pl.ds(pl.multiple_of(at * group, group), group)
+
+    def others():
+        return [lax.rem(r + distance, n_row) for distance in range(1, n_row)]
+
+    barrier = pltpu.get_barrier_semaphore()
+    for device in [to_col, to_core, to_side] + [{"row": at} for at in others()]:
+        pl.semaphore_signal(barrier, inc=1, device_id=device, device_id_type=MESH)
+    pl.semaphore_wait(barrier, 2 + n_row)
+
+    def x_copy(at):
+        src, dst = ((half(1 - c), own_slab.at[r, 1]), (half(c), far_slab.at[1]))[at]
+        return remote(slab_ref.at[src], dst, x_send.at[at], x_recv.at[at], to_col)
+
+    def own_copy(block, j, right, first=False):
+        src = slab_ref.at[half(c)] if first else own_slab.at[block, j]
+        return remote(
+            src, own_slab.at[block, j], own_send.at[block, j, 1 - right], own_recv.at[block, j],
+            {"row": r + 1 if right else r - 1},
+        )
+
+    def small_copy(at):
+        rows = pl.ds(pl.multiple_of(r * part, part), part)
+        return (
+            remote(upper_ref, fac.at[:, rows], small_send.at[at, 0], small_recv.at[r, 0], {"row": at}),
+            remote(map_ref, maps.at[r], small_send.at[at, 1], small_recv.at[r, 1], {"row": at}),
+        )
+
+    def small_arrival(at):
+        rows = pl.ds(pl.multiple_of(at * part, part), part)
+        return (
+            remote(upper_ref, fac.at[:, rows], small_send.at[at, 0], small_recv.at[at, 0], {"row": at}),
+            remote(map_ref, maps.at[at], small_send.at[at, 1], small_recv.at[at, 1], {"row": at}),
+        )
+
+    def both_ways(j, first):
+        for right in (1, 0):
+            @pl.when(r < n_row - 1 if right else r > 0)
+            def _(right=right):
+                own_copy(r, j, right, first).start()
+
+    x_copy(0).start()
+    for at in others():
+        for copy in small_copy(at):
+            copy.start()
+    both_ways(0, True)
+    x_copy(1).start()
+    locals_ = [
+        pltpu.make_async_copy(slab_ref.at[half(c)], own_slab.at[r, 0], here.at[0]),
+        pltpu.make_async_copy(slab_ref.at[half(1 - c)], far_slab.at[0], here.at[1]),
+    ]
+    loads = []
+    for slot, at in ((0, c), (1, 1 - c)):
+        for pole in range(n_pole):
+            loads.append(
+                pltpu.make_async_copy(
+                    window_ref.at[:, pole, :, half(at)], win.at[slot, pole], win_sem.at[slot, pole]
+                )
+            )
+    for copy in locals_ + loads:
+        copy.start()
+
+    maps[r] = map_ref[...]
+    fac[:, pl.ds(pl.multiple_of(r * part, part), part)] = upper_ref[...]
+    weight = jnp.float32(0.0)
+    for at in range(weights_ref.shape[0]):
+        weight += jnp.where(order_ref[0] == at, weights_ref[at], 0.0)
+    inner[...] = jnp.zeros_like(inner)
+
+    def reorder(slot, source, block, at):
+        def one(k, carry):
+            row = maps[block, pl.ds(k, 1), half(at)] - (block * n_col + at) * group
+            chosen = lax.broadcasted_iota(jnp.int32, (group, group), 0) == row
+            column = lax.rem(root_ref[0, k] + n_col - c, n_col)
+            rows = source[0]
+            for j in range(1, n_col):
+                rows = jnp.where(column == j, source[j], rows)
+            placed = lax.dot_general(
+                jnp.where(chosen, 1.0, 0.0).astype(rows.dtype), rows, (((0,), (0,)), ((), ())),
+                preferred_element_type=jnp.float32,
+            )
+            al[slot, :, pl.ds(pl.multiple_of(k * width, width), width)] = placed.astype(al.dtype)
+            return carry
+
+        lax.fori_loop(0, NS, one, 0)
+
+    near = jnp.minimum(r, n_row - 1 - r)
+    toward = jnp.where(r < n_row - 1 - r, 1, -1)
+
+    def block_at(step):
+        odd = lax.rem(step, 2)
+        zigzag = r + (2 * odd - 1) * ((step + 1) // 2)
+        return jnp.where(step <= 2 * near, zigzag, r + toward * (step - near))
+
+    def passes_on():
+        return (r > 0) & (r < n_row - 1)
+
+    def pass_on(step, j):
+        @pl.when(passes_on())
+        def _():
+            block = block_at(step)
+            own_copy(block, j, 1).wait_recv()
+
+            @pl.when(block < r)
+            def _():
+                own_copy(block, j, 1).start()
+
+            @pl.when(block > r)
+            def _():
+                own_copy(block, j, 0).start()
+
+    x_copy(0).wait_recv()
+    both_ways(1, False)
+    for copy in locals_:
+        copy.wait()
+    early = range(1, min(3, n_row))
+    for step in early:
+        pass_on(step, 0)
+    reorder(0, own_slab.at[r], r, c)
+    for copy in loads[:n_pole]:
+        copy.wait()
+
+    def first_pass(pole, carry):
+        left = win[0, pole].reshape(n_row * share, group)
+        y[pole] = jnp.dot(left, al[0], preferred_element_type=jnp.float32).reshape(n_row, share, NS * width)
+        return carry
+
+    lax.fori_loop(0, n_pole, first_pass, 0)
+    x_copy(1).wait_recv()
+    reorder(1, far_slab, r, 1 - c)
+    for copy in loads[n_pole:]:
+        copy.wait()
+    for at in others():
+        for copy in small_arrival(at):
+            copy.wait_recv()
+
+    n_half = n_row // 2
+
+    def core_copy(place, h):
+        pole = jnp.where(place == 0, 1 - side, side) * 2 + 1 - core
+        rows = pl.ds(h * n_half, n_half)
+        return remote(
+            y.at[pole, rows], core_in.at[place, rows], core_send.at[place, h], core_recv.at[place, h], to_core
+        )
+
+    def y_copy(h):
+        return (
+            remote(y_out.at[h], y_in.at[h], y_send.at[h, 0], y_recv.at[h, 0], to_side),
+            remote(y_out_top.at[h], y_in_top.at[h], y_send.at[h, 1], y_recv.at[h, 1], to_side),
+        )
+
+    def last_pass(i, carry):
+        kind, h = i // 2, lax.rem(i, 2)
+        place = kind // 2
+        pole = jnp.where(place == 0, 1 - side, side) * 2 + jnp.where(lax.rem(kind, 2) == 0, 1 - core, core)
+        rows = pl.ds(h * n_half, n_half)
+        left = win[1, pole, rows].reshape(n_half * share, group)
+        total = y[pole, rows].reshape(n_half * share, NS * width)
+        total = (total + jnp.dot(left, al[1], preferred_element_type=jnp.float32)) * -weight
+        columns, parts = [], []
+        for k in range(NS):
+            column = total[:, k * width : (k + 1) * width]
+            for m in range(k):
+                for piece in parts[m]:
+                    column = column - jnp.dot(piece, fac[pair_index(k, m)], preferred_element_type=jnp.float32)
+            columns.append(column)
+            parts.append(split(column))
+            y[pole, rows, :, k * width : (k + 1) * width] = column.reshape(n_half, share, width)
+
+        @pl.when(lax.rem(kind, 2) == 0)
+        def _():
+            core_copy(place, h).start()
+
+        @pl.when(kind == 1)
+        def _():
+            core_copy(0, h).wait_recv()
+            for at in range(n_half):
+                code, top = code_of(y[pole, h * n_half + at] + core_in[0, h * n_half + at])
+                y_out[h, at] = code
+                y_out_top[h, at] = top
+            for copy in y_copy(h):
+                copy.start()
+
+        @pl.when(i == 3)
+        def _():
+            for step in early:
+                pass_on(step, 1)
+
+        return carry
+
+    lax.fori_loop(0, 8, last_pass, 0)
+    for step in range(3, n_row):
+        for j in range(2):
+            pass_on(step, j)
+
+    mine = side * 2 + core
+
+    def z_copy(at, slot):
+        return (
+            remote(z_out.at[at], z_in.at[slot], z_send.at[at, 0], z_recv.at[slot, 0], {"row": at}),
+            remote(z_out_top.at[at], z_in_top.at[slot], z_send.at[at, 1], z_recv.at[slot, 1], {"row": at}),
+        )
+
+    def finish(h):
+        core_copy(1, h).wait_recv()
+        for copy in y_copy(h):
+            copy.wait_recv()
+        for at in range(n_half):
+            row = h * n_half + at
+            total = y[mine, row] + core_in[1, row] + value_of(y_in[h, at], y_in_top[h, at])
+            core_in[1, row] = total
+            code, top = code_of(total)
+            z_out[row] = code
+            z_out_top[row] = top
+
+            @pl.when(r != row)
+            def _(row=row):
+                for copy in z_copy(row, r):
+                    copy.start()
+
+    def gather_inner(step, carry):
+        block = block_at(step)
+
+        @pl.when(step > 0)
+        def _():
+            @pl.when((r == 0) | (r == n_row - 1))
+            def _():
+                for j in range(2):
+                    own_copy(block, j, 1).wait_recv()
+
+            reorder(1, own_slab.at[block], block, c)
+
+        slot = jnp.minimum(step, 1)
+        for m in range(NS):
+            column = jnp.concatenate(
+                [y[pole, block, :, m * width : (m + 1) * width] for pole in range(n_pole)]
+            )
+            pieces = split(column)
+            for k in range(m, NS):
+                rows = al[slot, :, k * width : (k + 1) * width]
+                for piece in pieces:
+                    inner[k * (k + 1) // 2 + m] += lax.dot_general(
+                        rows, piece, (((0,), (0,)), ((), ())), preferred_element_type=jnp.float32
+                    )
+
+        @pl.when(step == n_row - 2)
+        def _():
+            finish(0)
+            finish(1)
+
+        return carry
+
+    lax.fori_loop(0, n_row, gather_inner, 0)
+
+    spread[...] = jnp.zeros_like(spread)
+    spread[:, pl.ds(pl.multiple_of(r * part, part), part)] = diag_ref[...] * (weight * (1.0 / n_col))
+    wide = [fac[e].astype(jnp.float32) for e in range(fac.shape[0])]
+    diagonals, crossed = [], {}
+
+    def inverse_block(m, n):
+        if m == n:
+            return diagonals[m]
+        return crossed[m, n] if m < n else crossed[n, m].T
+
+    for k in range(NS):
+        diagonal = spread[k] - inner[k * (k + 1) // 2 + k]
+        for m in range(k):
+            y_block = inner[k * (k + 1) // 2 + m].T
+            for n in range(k):
+                y_block = y_block + precise(inverse_block(m, n), wide[pair_index(k, n)])
+            crossed[m, k] = -y_block
+            diagonal = diagonal + precise(wide[pair_index(k, m)].T, y_block)
+        diagonals.append(diagonal)
+        blocks = diagonal.reshape(n_row, n_pole, depth, width)
+        for pole in range(n_pole):
+            g_all[pole, :, :, k * width : (k + 1) * width] = blocks[:, pole]
+
+    def gc_copy(at):
+        return remote(g_all.at[at * 2 + 1 - core], g_core.at[at], gc_send.at[at], gc_recv.at[at], to_core)
+
+    for at in range(2):
+        gc_copy(at).start()
+    gc_copy(1 - side).wait_recv()
+    g_half[...] = g_all[(1 - side) * 2 + core] + g_core[1 - side]
+    gy_copy = remote(g_half, g_y, gy_send, gy_recv, to_side)
+    gy_copy.start()
+    gc_copy(side).wait_recv()
+    gy_copy.wait_recv()
+    g_sum[...] = g_all[mine] + g_core[side] + g_y[...]
+
+    def gz_copy(at, slot):
+        return remote(g_sum.at[at], g_z.at[slot], gz_send.at[at], gz_recv.at[slot], {"row": at})
+
+    for at in others():
+        gz_copy(at, r).start()
+
+    total = core_in[1, r]
+    for at in others():
+        for copy in z_copy(at, at):
+            copy.wait_recv()
+        total = total + value_of(z_in[at], z_in_top[at])
+    for k in range(NS):
+        columns_ref[k] = total[:, k * width : (k + 1) * width]
+
+    total = g_sum[r]
+    for at in others():
+        gz_copy(at, at).wait_recv()
+        total = total + g_z[at]
+    g_last[...] = total
+    gx_copy = remote(g_last, g_x, gx_send, gx_recv, to_col)
+    gx_copy.start()
+    gx_copy.wait_recv()
+    total = total + g_x[...]
+    for k in range(NS):
+        diagonal_ref[k] = total[:, k * width : (k + 1) * width]
+
+    for at in range(2):
+        x_copy(at).wait_send()
+        gc_copy(at).wait_send()
+        for h in range(2):
+            core_copy(at, h).wait_send()
+        for copy in y_copy(at):
+            copy.wait_send()
+    gy_copy.wait_send()
+    gx_copy.wait_send()
+    for at in others():
+        for copy in small_copy(at) + z_copy(at, r):
+            copy.wait_send()
+        gz_copy(at, r).wait_send()
+    for j in range(2):
+        for right in (1, 0):
+            @pl.when(r < n_row - 1 if right else r > 0)
+            def _(right=right, j=j):
+                own_copy(r, j, right, j == 0).wait_send()
+
+        for step in range(1, n_row):
+            @pl.when(passes_on())
+            def _(step=step, j=j):
+                block = block_at(step)
+
+                @pl.when(block < r)
+                def _():
+                    own_copy(block, j, 1).wait_send()
+
+                @pl.when(block > r)
+                def _():
+                    own_copy(block, j, 0).wait_send()
+
+
+def fused(window, panels, row_map, panel_root, upper_blocks, diag_inverse, weights, pole_order):
+    n_row, n_col, n_pole = (lax.axis_size(name) for name in ("row", "col", "pole"))
+    slab = panels[0, 0]
+    width = slab.shape[1]
+    group = window.shape[1] // n_row
+    share = group // n_pole
+    depth = width // (n_row * n_pole)
+    pairs = upper_blocks.shape[1]
+    total = NS * width
+    rows = window[0].reshape(n_row, n_pole, share, n_col * group)
+    smem, vmem, hbm = (pl.BlockSpec(memory_space=m) for m in (pltpu.SMEM, pltpu.VMEM, pl.ANY))
+    bf16, f32, i16, i32 = jnp.bfloat16, jnp.float32, jnp.int16, jnp.int32
+    dma = pltpu.SemaphoreType.DMA
+    columns, diagonal = pl.pallas_call(
+        fused_kernel,
+        out_shape=(
+            jax.ShapeDtypeStruct((NS, share, width), f32),
+            jax.ShapeDtypeStruct((NS, depth, width), f32),
+        ),
+        in_specs=[smem, smem, smem, hbm, hbm, vmem, vmem, vmem],
+        out_specs=(vmem, vmem),
+        scratch_shapes=[
+            pltpu.VMEM((n_col, n_pole, n_row, share, group), bf16),
+            pltpu.VMEM((n_row, n_col, group, width), bf16),
+            pltpu.VMEM((n_col, group, width), bf16),
+            pltpu.VMEM((n_row, NS, n_col * group), i32),
+            pltpu.VMEM((pairs, width, width), bf16),
+            pltpu.VMEM((2, group, total), bf16),
+            pltpu.VMEM((n_pole, n_row, share, total), f32),
+            pltpu.VMEM((2, n_row, share, total), f32),
+            pltpu.VMEM((2, n_row // 2, share, total), i16),
+            pltpu.VMEM((2, n_row // 2, 1, total), f32),
+            pltpu.VMEM((2, n_row // 2, share, total), i16),
+            pltpu.VMEM((2, n_row // 2, 1, total), f32),
+            pltpu.VMEM((n_row, share, total), i16),
+            pltpu.VMEM((n_row, 1, total), f32),
+            pltpu.VMEM((n_row, share, total), i16),
+            pltpu.VMEM((n_row, 1, total), f32),
+            pltpu.VMEM((NS * (NS + 1) // 2, width, width), f32),
+            pltpu.VMEM((NS, width, width), f32),
+            pltpu.VMEM((n_pole, n_row, depth, total), f32),
+            pltpu.VMEM((2, n_row, depth, total), f32),
+            pltpu.VMEM((n_row, depth, total), f32),
+            pltpu.VMEM((n_row, depth, total), f32),
+            pltpu.VMEM((n_row, depth, total), f32),
+            pltpu.VMEM((n_row, depth, total), f32),
+            pltpu.VMEM((depth, total), f32),
+            pltpu.VMEM((depth, total), f32),
+            dma((2,)), dma((2,)), dma((2,)), dma((n_col, n_pole)),
+            dma((n_row, 2, 2)), dma((n_row, 2)), dma((n_row, 2)), dma((n_row, 2)),
+            dma((2, 2)), dma((2, 2)), dma((2, 2)), dma((2, 2)), dma((n_row, 2)), dma((n_row, 2)),
+            dma((2,)), dma((2,)), dma, dma, dma((n_row,)), dma((n_row,)), dma, dma,
+        ],
+        compiler_params=pltpu.CompilerParams(
+            collective_id=0, has_side_effects=True, vmem_limit_bytes=67043328
+        ),
+        name="fused",
+    )(weights, pole_order, panel_root, rows, slab, row_map, upper_blocks[0], diag_inverse[0])
+    return columns[:, None], diagonal
+
+
+def fits(mesh, window, upper_blocks):
+    n_row, n_col, n_pole = (mesh.shape[name] for name in ("row", "col", "pole"))
+    share = window.shape[1] // (n_row * n_col * n_pole)
+    depth = upper_blocks.shape[3] // (n_row * n_pole)
+    return n_col == 2 and n_pole == 4 and n_row % 2 == 0 and share % 128 == 0 and depth % 8 == 0
+
+
 def solution(mesh):
-    return jax.shard_map(
+    step = jax.shard_map(
         staged,
         mesh=mesh,
         in_specs=(
@@ -383,3 +837,26 @@
         out_specs=(P(None, "col", ("row", "pole"), None), P(None, ("row", "pole"), None)),
         check_vma=False,
     )
+    staged_step = step
+    fused_step = jax.shard_map(
+        fused,
+        mesh=mesh,
+        in_specs=(
+            P("pole", "col", "row"),
+            P("pole", "col", "row", None),
+            P(None, "row"),
+            P("pole", None),
+            P("pole", None, "row", None),
+            P("pole", None, "row", None),
+            P(),
+            P("pole"),
+        ),
+        out_specs=(P(None, "col", ("row", "pole"), None), P(None, ("row", "pole"), None)),
+        check_vma=False,
+    )
+
+    def chosen(window, panels, row_map, panel_root, upper_blocks, *rest):
+        one = fused_step if fits(mesh, window, upper_blocks) else staged_step
+        return one(window, panels, row_map, panel_root, upper_blocks, *rest)
+
+    return chosen

time: 303 us -> 129 us (0.43)
  waiting for transfers between devices: 121 us -> 0 us
  starting transfers between devices: 63.6 us -> 0 us
  Pallas kernels: 70.3 us -> 123 us
  other arithmetic: 28.4 us -> 0 us
  local copies, waits for them, and re-layouts: 10.6 us -> 3.48 us
  matrix products: 4.51 us -> 0 us
    ppermute x34 -> x0, waiting for transfers between devices: 121 us -> none  [the longest x25 94.6 us: shift(): lax.ppermute(block, axis_name, [(i, (i + distance) % size) for i in range...]
    ppermute x34 -> x0, starting transfers between devices: 63.6 us -> none  [the longest x25 55.3 us: shift(): lax.ppermute(block, axis_name, [(i, (i + distance) % size) for i in range...]
    pallas_call x6 -> x1, Pallas kernels: 70.3 us -> 123 us  [fused(): pl.pallas_call(fused_kernel, out_shape=(jax.ShapeDtypeStruct((NS, share,...]
    reduce_max x2 -> x0, other arithmetic: 7.3 us -> none  [encode(): top = jnp.maximum(jnp.max(jnp.abs(value), axis=-1), 1e-30)]
    another operation x7 -> x0, other arithmetic: 7.29 us -> none  [the longest x2 4.86 us: staged(): stacked_own = jnp.stack([jnp.stack(blocks) for blocks in own_slab])]
    dot_general x8 -> x0, matrix products: 4.51 us -> none  [precise(): jnp.dot(left, right, precision=lax.Precision.HIGHEST, preferred_element_t...]
    convert_element_type x7 -> x0, other arithmetic: 4.33 us -> none  [the longest x3 2.89 us: encode(): jnp.round(value * (32000.0 / top)[..., None]).astype(jnp.int16)]
    dynamic_slice x2 -> x0, local copies, waits for them, and re-layouts: 3.82 us -> none  [the longest x1 1.92 us: staged(): lax.dynamic_slice_in_dim(slab, own_start, group, 0)]
  transfers between devices with their start and end apart: 34 -> 0, of which waited for: 15 -> 0; matrix products, arithmetic and copies ran while one was open for 11% -> 0% of each run, Pallas kernels for 16% -> 0%
where the time goes in v1:
time: 129 us; the launch traced here: 128 us
  Pallas kernels  123 us (95%)
  local copies, waits for them, and re-layouts  3.48 us (3%)
  between operations  1.29 us (1%)
    pallas_call x1, Pallas kernels, fused(): pl.pallas_call(fused_kernel, out_shape=(jax.ShapeDtypeStruct((NS, share,...  123 us
    unnamed x2, local copies, waits for them, and re-layouts  3.48 us

profile of v1, /device:TPU:0, one launch (start us, length us, event | category | flops | bytes accessed | tf_op | source)
XLA Modules:
  0.0 127.8 jit_solution(12025328803458728304)
XLA Ops:
  1.3 123.0 %fused.1 = (f32[3,256,256]{2,1,0:T(8,128)}, f32[3,16,256]{2,1,0:T(8,128)}) custom-call(f32[4]{0:T(128)} %weights_ref.1, s32[1]{0:T(128)S(6)} %copy.13.order_ref, s32[1,3]{1,0:T(1,128)} %root_ref.1, bf16[4,4,256,2048]{3,2,1,0:T(8,128)(2,1)} %bitcast.7, bf16[2048,256]{1,0:T(8,128)(2,1)} %bitcast.8, s32[3,2048]{1,0:T(4,128)} %map_ref.1, ...), custom_call_target="tpu_custom_call" | custom-call | tf_op jit(solution)/shard_map/fused/pallas_call | solution.py:768
  124.3 2.1 %copy.14 = f32[3,1,256,256]{3,2,1,0:T(8,128)} copy(f32[3,1,256,256]{3,2,1,0:T(8,128)} %bitcast.9) | data formatting | bytes 1572864
  126.4 1.4 %copy.15 = f32[3,16,256]{2,1,0:T(8,128)} copy(f32[3,16,256]{2,1,0:T(8,128)} %get-tuple-element.11) | data formatting | bytes 98304

commit v2 on v1

--- a/solution.py
+++ b/solution.py
@@ -368,11 +368,13 @@
 
 MESH = pl.DeviceIdType.MESH
 LEVELS = 32000.0
+NEAREST = 12582912.0
 
 
 def code_of(value):
     top = jnp.maximum(jnp.max(jnp.abs(value), axis=0, keepdims=True), 1e-30)
-    return jnp.round(value * (LEVELS / top)).astype(jnp.int32).astype(jnp.int16), top
+    nearest = (value * (LEVELS / top) + NEAREST) - NEAREST
+    return nearest.astype(jnp.int32).astype(jnp.int16), top
 
 
 def value_of(code, top):
@@ -383,7 +385,8 @@
     weights_ref, order_ref, root_ref, window_ref, slab_ref, map_ref, upper_ref, diag_ref,
     columns_ref, diagonal_ref,
     win, own_slab, far_slab, maps, fac, al, y, core_in, y_out, y_out_top, y_in, y_in_top,
-    z_out, z_out_top, z_in, z_in_top, inner, spread, g_all, g_core, g_half, g_y, g_sum, g_z, g_x, g_last,
+    z_out, z_out_top, z_in, z_in_top, inner, spread, g_all, g_core, g_out, g_out_top, g_in, g_in_top,
+    g_sum, gz_out, gz_out_top, gz_in, gz_in_top, g_x, g_last,
     x_send, x_recv, here, win_sem, own_send, own_recv, small_send, small_recv,
     core_send, core_recv, y_send, y_recv, z_send, z_recv,
     gc_send, gc_recv, gy_send, gy_recv, gz_send, gz_recv, gx_send, gx_recv,
@@ -428,14 +431,20 @@
         rows = pl.ds(pl.multiple_of(r * part, part), part)
         return (
             remote(upper_ref, fac.at[:, rows], small_send.at[at, 0], small_recv.at[r, 0], {"row": at}),
-            remote(map_ref, maps.at[r], small_send.at[at, 1], small_recv.at[r, 1], {"row": at}),
+            remote(
+                map_ref.at[:, half(c)], maps.at[r, :, half(c)], small_send.at[at, 1], small_recv.at[r, 1],
+                {"row": at},
+            ),
         )
 
     def small_arrival(at):
         rows = pl.ds(pl.multiple_of(at * part, part), part)
         return (
             remote(upper_ref, fac.at[:, rows], small_send.at[at, 0], small_recv.at[at, 0], {"row": at}),
-            remote(map_ref, maps.at[at], small_send.at[at, 1], small_recv.at[at, 1], {"row": at}),
+            remote(
+                map_ref.at[:, half(c)], maps.at[at, :, half(c)], small_send.at[at, 1], small_recv.at[at, 1],
+                {"row": at},
+            ),
         )
 
     def both_ways(j, first):
@@ -445,11 +454,11 @@
                 own_copy(r, j, right, first).start()
 
     x_copy(0).start()
+    both_ways(0, True)
+    x_copy(1).start()
     for at in others():
         for copy in small_copy(at):
             copy.start()
-    both_ways(0, True)
-    x_copy(1).start()
     locals_ = [
         pltpu.make_async_copy(slab_ref.at[half(c)], own_slab.at[r, 0], here.at[0]),
         pltpu.make_async_copy(slab_ref.at[half(1 - c)], far_slab.at[0], here.at[1]),
@@ -519,9 +528,9 @@
     for copy in locals_:
         copy.wait()
     early = range(1, min(3, n_row))
+    reorder(0, own_slab.at[r], r, c)
     for step in early:
         pass_on(step, 0)
-    reorder(0, own_slab.at[r], r, c)
     for copy in loads[:n_pole]:
         copy.wait()
 
@@ -594,10 +603,6 @@
         return carry
 
     lax.fori_loop(0, 8, last_pass, 0)
-    for step in range(3, n_row):
-        for j in range(2):
-            pass_on(step, j)
-
     mine = side * 2 + core
 
     def z_copy(at, slot):
@@ -625,6 +630,11 @@
 
     def gather_inner(step, carry):
         block = block_at(step)
+
+        @pl.when(step == 1)
+        def _():
+            for later in range(3, n_row):
+                pass_on(later, 0)
 
         @pl.when(step > 0)
         def _():
@@ -650,6 +660,8 @@
 
         @pl.when(step == n_row - 2)
         def _():
+            for later in range(3, n_row):
+                pass_on(later, 1)
             finish(0)
             finish(1)
 
@@ -686,18 +698,34 @@
     for at in range(2):
         gc_copy(at).start()
     gc_copy(1 - side).wait_recv()
-    g_half[...] = g_all[(1 - side) * 2 + core] + g_core[1 - side]
-    gy_copy = remote(g_half, g_y, gy_send, gy_recv, to_side)
-    gy_copy.start()
+    away = g_all[(1 - side) * 2 + core] + g_core[1 - side]
+    g_out[...], g_out_top[...] = code_of(away.reshape(n_row * depth, NS * width))
+
+    def gy_copies():
+        return (
+            remote(g_out, g_in, gy_send.at[0], gy_recv.at[0], to_side),
+            remote(g_out_top, g_in_top, gy_send.at[1], gy_recv.at[1], to_side),
+        )
+
+    for copy in gy_copies():
+        copy.start()
     gc_copy(side).wait_recv()
-    gy_copy.wait_recv()
-    g_sum[...] = g_all[mine] + g_core[side] + g_y[...]
+    for copy in gy_copies():
+        copy.wait_recv()
+    come = value_of(g_in[...], g_in_top[...]).reshape(n_row, depth, NS * width)
+    g_sum[...] = g_all[mine] + g_core[side] + come
+    for at in range(n_row):
+        gz_out[at], gz_out_top[at] = code_of(g_sum[at])
 
     def gz_copy(at, slot):
-        return remote(g_sum.at[at], g_z.at[slot], gz_send.at[at], gz_recv.at[slot], {"row": at})
+        return (
+            remote(gz_out.at[at], gz_in.at[slot], gz_send.at[at, 0], gz_recv.at[slot, 0], {"row": at}),
+            remote(gz_out_top.at[at], gz_in_top.at[slot], gz_send.at[at, 1], gz_recv.at[slot, 1], {"row": at}),
+        )
 
     for at in others():
-        gz_copy(at, r).start()
+        for copy in gz_copy(at, r):
+            copy.start()
 
     total = core_in[1, r]
     for at in others():
@@ -709,8 +737,9 @@
 
     total = g_sum[r]
     for at in others():
-        gz_copy(at, at).wait_recv()
-        total = total + g_z[at]
+        for copy in gz_copy(at, at):
+            copy.wait_recv()
+        total = total + value_of(gz_in[at], gz_in_top[at])
     g_last[...] = total
     gx_copy = remote(g_last, g_x, gx_send, gx_recv, to_col)
     gx_copy.start()
@@ -726,12 +755,12 @@
             core_copy(at, h).wait_send()
         for copy in y_copy(at):
             copy.wait_send()
-    gy_copy.wait_send()
+    for copy in gy_copies():
+        copy.wait_send()
     gx_copy.wait_send()
     for at in others():
-        for copy in small_copy(at) + z_copy(at, r):
+        for copy in small_copy(at) + z_copy(at, r) + gz_copy(at, r):
             copy.wait_send()
-        gz_copy(at, r).wait_send()
     for j in range(2):
         for right in (1, 0):
             @pl.when(r < n_row - 1 if right else r > 0)
@@ -794,16 +823,21 @@
             pltpu.VMEM((NS, width, width), f32),
             pltpu.VMEM((n_pole, n_row, depth, total), f32),
             pltpu.VMEM((2, n_row, depth, total), f32),
+            pltpu.VMEM((n_row * depth, total), i16),
+            pltpu.VMEM((1, total), f32),
+            pltpu.VMEM((n_row * depth, total), i16),
+            pltpu.VMEM((1, total), f32),
             pltpu.VMEM((n_row, depth, total), f32),
-            pltpu.VMEM((n_row, depth, total), f32),
-            pltpu.VMEM((n_row, depth, total), f32),
-            pltpu.VMEM((n_row, depth, total), f32),
+            pltpu.VMEM((n_row, depth, total), i16),
+            pltpu.VMEM((n_row, 1, total), f32),
+            pltpu.VMEM((n_row, depth, total), i16),
+            pltpu.VMEM((n_row, 1, total), f32),
             pltpu.VMEM((depth, total), f32),
             pltpu.VMEM((depth, total), f32),
             dma((2,)), dma((2,)), dma((2,)), dma((n_col, n_pole)),
             dma((n_row, 2, 2)), dma((n_row, 2)), dma((n_row, 2)), dma((n_row, 2)),
             dma((2, 2)), dma((2, 2)), dma((2, 2)), dma((2, 2)), dma((n_row, 2)), dma((n_row, 2)),
-            dma((2,)), dma((2,)), dma, dma, dma((n_row,)), dma((n_row,)), dma, dma,
+            dma((2,)), dma((2,)), dma((2,)), dma((2,)), dma((n_row, 2)), dma((n_row, 2)), dma, dma,
         ],
         compiler_params=pltpu.CompilerParams(
             collective_id=0, has_side_effects=True, vmem_limit_bytes=67043328

time: 129 us -> 127 us (0.984)
  Pallas kernels: 123 us -> 121 us
    pallas_call x1, Pallas kernels: 123 us -> 121 us  [fused(): pl.pallas_call(fused_kernel, out_shape=(jax.ShapeDtypeStruct((NS, share,...]
where the time goes in v2:
time: 127 us; the launch traced here: 126 us
  Pallas kernels  121 us (95%)
  local copies, waits for them, and re-layouts  3.48 us (3%)
  between operations  1.29 us (1%)
    pallas_call x1, Pallas kernels, fused(): pl.pallas_call(fused_kernel, out_shape=(jax.ShapeDtypeStruct((NS, share,...  121 us
    unnamed x2, local copies, waits for them, and re-layouts  3.48 us

profile of v2, /device:TPU:0, one launch (start us, length us, event | category | flops | bytes accessed | tf_op | source)
XLA Modules:
  0.0 125.7 jit_solution(13171657999618105987)
XLA Ops:
  1.3 120.9 %fused.1 = (f32[3,256,256]{2,1,0:T(8,128)}, f32[3,16,256]{2,1,0:T(8,128)}) custom-call(f32[4]{0:T(128)} %weights_ref.1, s32[1]{0:T(128)S(6)} %copy.13.order_ref, s32[1,3]{1,0:T(1,128)} %root_ref.1, bf16[4,4,256,2048]{3,2,1,0:T(8,128)(2,1)} %bitcast.7, bf16[2048,256]{1,0:T(8,128)(2,1)} %bitcast.8, s32[3,2048]{1,0:T(4,128)} %map_ref.1, ...), custom_call_target="tpu_custom_call" | custom-call | tf_op jit(solution)/shard_map/fused/pallas_call | solution.py:797
  122.2 2.1 %copy.14 = f32[3,1,256,256]{3,2,1,0:T(8,128)} copy(f32[3,1,256,256]{3,2,1,0:T(8,128)} %bitcast.9) | data formatting | bytes 1572864
  124.3 1.4 %copy.15 = f32[3,16,256]{2,1,0:T(8,128)} copy(f32[3,16,256]{2,1,0:T(8,128)} %get-tuple-element.11) | data formatting | bytes 98304

commit v3 on v2

--- a/solution.py
+++ b/solution.py
@@ -275,9 +275,7 @@
     packed_map = jnp.pad(packed_map, (0, -packed_map.shape[0] % width)).reshape(-1, width)
     part_rows = upper_blocks.shape[2]
     pairs = upper_blocks.shape[1]
-    gathered = shift_gather(
-        jnp.concatenate([upper_blocks[0].reshape(-1, width), packed_map]), "row"
-    )
+    gathered = shift_gather(jnp.concatenate([upper_blocks[0].reshape(-1, width), packed_map]), "row")
     own_slab = [shift_gather(lax.dynamic_slice_in_dim(slab, own_start, group, 0), "row")]
     factors = jnp.zeros((pairs, part_rows * n_row, width), upper_blocks.dtype)
     maps = []
@@ -292,10 +290,7 @@
     stacked_slabs = jnp.stack(slabs).reshape(n_col, n_col, group, width)
     stacked_map = jnp.stack([local_map[:, c * group : (c + 1) * group] for c in range(n_col)])
     aligned = reorder(slab_index, stacked_map, stacked_slabs)
-    own_slab += [
-        shift_gather(lax.dynamic_slice_in_dim(other, own_start, group, 0), "row")
-        for other in slabs[1:]
-    ]
+    own_slab += [shift_gather(lax.dynamic_slice_in_dim(other, own_start, group, 0), "row") for other in slabs[1:]]
 
     window_rows = window_block.reshape(n_row * n_pole, share, window_block.shape[1])
     scale = (-pole_weight).reshape(1)
@@ -563,8 +558,12 @@
             remote(y_out_top.at[h], y_in_top.at[h], y_send.at[h, 1], y_recv.at[h, 1], to_side),
         )
 
+    low = r < n_half
+    far_half = jnp.where(low, 1, 0)
+
     def last_pass(i, carry):
-        kind, h = i // 2, lax.rem(i, 2)
+        kind = i // 2
+        h = jnp.where(lax.rem(i, 2) == 0, far_half, 1 - far_half)
         place = kind // 2
         pole = jnp.where(place == 0, 1 - side, side) * 2 + jnp.where(lax.rem(kind, 2) == 0, 1 - core, core)
         rows = pl.ds(h * n_half, n_half)
@@ -605,10 +604,11 @@
     lax.fori_loop(0, 8, last_pass, 0)
     mine = side * 2 + core
 
-    def z_copy(at, slot):
+    def z_copy(at, way):
+        device = {"row": r + 1 - 2 * way}
         return (
-            remote(z_out.at[at], z_in.at[slot], z_send.at[at, 0], z_recv.at[slot, 0], {"row": at}),
-            remote(z_out_top.at[at], z_in_top.at[slot], z_send.at[at, 1], z_recv.at[slot, 1], {"row": at}),
+            remote(z_out.at[at], z_in.at[way, at], z_send.at[at, 0], z_recv.at[way, at, 0], device),
+            remote(z_out_top.at[at], z_in_top.at[way, at], z_send.at[at, 1], z_recv.at[way, at, 1], device),
         )
 
     def finish(h):
@@ -617,16 +617,28 @@
             copy.wait_recv()
         for at in range(n_half):
             row = h * n_half + at
-            total = y[mine, row] + core_in[1, row] + value_of(y_in[h, at], y_in_top[h, at])
-            core_in[1, row] = total
-            code, top = code_of(total)
-            z_out[row] = code
-            z_out_top[row] = top
-
-            @pl.when(r != row)
-            def _(row=row):
-                for copy in z_copy(row, r):
-                    copy.start()
+            core_in[1, row] = y[mine, row] + core_in[1, row] + value_of(y_in[h, at], y_in_top[h, at])
+
+    def add_come(at, way):
+        @pl.when(jnp.where(way == 0, r, n_row - 1 - r) > 0)
+        def _():
+            for copy in z_copy(at, way):
+                copy.wait_recv()
+            core_in[1, at] = core_in[1, at] + value_of(z_in[way, at], z_in_top[way, at])
+
+    def forward(at, way):
+        @pl.when(jnp.where(way == 0, at - r, r - at) > 0)
+        def _():
+            add_come(at, way)
+            z_out[at], z_out_top[at] = code_of(core_in[1, at])
+            for copy in z_copy(at, way):
+                copy.start()
+
+    def far(n):
+        forward(jnp.where(low, n_row - 1 - n, n), jnp.where(low, 0, 1))
+
+    def close(n):
+        forward(jnp.where(low, n, n_row - 1 - n), jnp.where(low, 1, 0))
 
     def gather_inner(step, carry):
         block = block_at(step)
@@ -662,12 +674,29 @@
         def _():
             for later in range(3, n_row):
                 pass_on(later, 1)
-            finish(0)
-            finish(1)
+            finish(far_half)
+
+            @pl.when(jnp.logical_not(passes_on()))
+            def _():
+                for n in range(n_half):
+                    far(n)
+                finish(1 - far_half)
+                for n in range(n_half, n_row - 1):
+                    far(n)
 
         return carry
 
     lax.fori_loop(0, n_row, gather_inner, 0)
+
+    @pl.when(passes_on())
+    def _():
+        far(0)
+        finish(1 - far_half)
+        for n in range(1, n_row - 1):
+            far(n)
+        for n in range(n_row - 1):
+            close(n)
+
 
     spread[...] = jnp.zeros_like(spread)
     spread[:, pl.ds(pl.multiple_of(r * part, part), part)] = diag_ref[...] * (weight * (1.0 / n_col))
@@ -727,11 +756,9 @@
         for copy in gz_copy(at, r):
             copy.start()
 
+    for way in range(2):
+        add_come(r, way)
     total = core_in[1, r]
-    for at in others():
-        for copy in z_copy(at, at):
-            copy.wait_recv()
-        total = total + value_of(z_in[at], z_in_top[at])
     for k in range(NS):
         columns_ref[k] = total[:, k * width : (k + 1) * width]
 
@@ -759,7 +786,7 @@
         copy.wait_send()
     gx_copy.wait_send()
     for at in others():
-        for copy in small_copy(at) + z_copy(at, r) + gz_copy(at, r):
+        for copy in small_copy(at) + z_copy(at, 0) + gz_copy(at, r):
             copy.wait_send()
     for j in range(2):
         for right in (1, 0):
@@ -817,8 +844,8 @@
             pltpu.VMEM((2, n_row // 2, 1, total), f32),
             pltpu.VMEM((n_row, share, total), i16),
             pltpu.VMEM((n_row, 1, total), f32),
-            pltpu.VMEM((n_row, share, total), i16),
-            pltpu.VMEM((n_row, 1, total), f32),
+            pltpu.VMEM((2, n_row, share, total), i16),
+            pltpu.VMEM((2, n_row, 1, total), f32),
             pltpu.VMEM((NS * (NS + 1) // 2, width, width), f32),
             pltpu.VMEM((NS, width, width), f32),
             pltpu.VMEM((n_pole, n_row, depth, total), f32),
@@ -836,7 +863,7 @@
             pltpu.VMEM((depth, total), f32),
             dma((2,)), dma((2,)), dma((2,)), dma((n_col, n_pole)),
             dma((n_row, 2, 2)), dma((n_row, 2)), dma((n_row, 2)), dma((n_row, 2)),
-            dma((2, 2)), dma((2, 2)), dma((2, 2)), dma((2, 2)), dma((n_row, 2)), dma((n_row, 2)),
+            dma((2, 2)), dma((2, 2)), dma((2, 2)), dma((2, 2)), dma((n_row, 2)), dma((2, n_row, 2)),
             dma((2,)), dma((2,)), dma((2,)), dma((2,)), dma((n_row, 2)), dma((n_row, 2)), dma, dma,
         ],
         compiler_params=pltpu.CompilerParams(

time: 127 us -> 110 us (0.87)
  Pallas kernels: 121 us -> 105 us
    pallas_call x1, Pallas kernels: 121 us -> 105 us  [fused(): pl.pallas_call(fused_kernel, out_shape=(jax.ShapeDtypeStruct((NS, share,...]
where the time goes in v3:
time: 110 us
  Pallas kernels  105 us (95%)
  local copies, waits for them, and re-layouts  3.48 us (3%)
  between operations  1.29 us (1%)
    pallas_call x1, Pallas kernels, fused(): pl.pallas_call(fused_kernel, out_shape=(jax.ShapeDtypeStruct((NS, share,...  105 us
    unnamed x2, local copies, waits for them, and re-layouts  3.48 us

profile of v3, /device:TPU:0, one launch (start us, length us, event | category | flops | bytes accessed | tf_op | source)
XLA Modules:
  0.0 110.0 jit_solution(993305563679486057)
XLA Ops:
  1.3 105.2 %fused.1 = (f32[3,256,256]{2,1,0:T(8,128)}, f32[3,16,256]{2,1,0:T(8,128)}) custom-call(f32[4]{0:T(128)} %weights_ref.1, s32[1]{0:T(128)S(6)} %copy.13.order_ref, s32[1,3]{1,0:T(1,128)} %root_ref.1, bf16[4,4,256,2048]{3,2,1,0:T(8,128)(2,1)} %bitcast.7, bf16[2048,256]{1,0:T(8,128)(2,1)} %bitcast.8, s32[3,2048]{1,0:T(4,128)} %map_ref.1, ...), custom_call_target="tpu_custom_call" | custom-call | tf_op jit(solution)/shard_map/fused/pallas_call | solution.py:824
  106.5 2.1 %copy.14 = f32[3,1,256,256]{3,2,1,0:T(8,128)} copy(f32[3,1,256,256]{3,2,1,0:T(8,128)} %bitcast.9) | data formatting | bytes 1572864
  108.5 1.4 %copy.15 = f32[3,16,256]{2,1,0:T(8,128)} copy(f32[3,16,256]{2,1,0:T(8,128)} %get-tuple-element.11) | data formatting | bytes 98304

commit v4 on v3

--- a/solution.py
+++ b/solution.py
@@ -382,7 +382,7 @@
     win, own_slab, far_slab, maps, fac, al, y, core_in, y_out, y_out_top, y_in, y_in_top,
     z_out, z_out_top, z_in, z_in_top, inner, spread, g_all, g_core, g_out, g_out_top, g_in, g_in_top,
     g_sum, gz_out, gz_out_top, gz_in, gz_in_top, g_x, g_last,
-    x_send, x_recv, here, win_sem, own_send, own_recv, small_send, small_recv,
+    x_send, x_recv, here, win_sem, own_send, own_recv, small_send, small_recv, share_send, share_recv,
     core_send, core_recv, y_send, y_recv, z_send, z_recv,
     gc_send, gc_recv, gy_send, gy_recv, gz_send, gz_recv, gx_send, gx_recv,
 ):
@@ -422,25 +422,25 @@
             {"row": r + 1 if right else r - 1},
         )
 
-    def small_copy(at):
-        rows = pl.ds(pl.multiple_of(r * part, part), part)
+    piece = part // n_col
+
+    def small_copy(at, sender):
+        mine_at = pl.ds(pl.multiple_of(c * piece, piece), piece)
+        rows = pl.ds(pl.multiple_of(sender * part + c * piece, piece), piece)
         return (
-            remote(upper_ref, fac.at[:, rows], small_send.at[at, 0], small_recv.at[r, 0], {"row": at}),
             remote(
-                map_ref.at[:, half(c)], maps.at[r, :, half(c)], small_send.at[at, 1], small_recv.at[r, 1],
+                upper_ref.at[:, mine_at], fac.at[:, rows], small_send.at[at, 0], small_recv.at[sender, 0],
                 {"row": at},
             ),
-        )
-
-    def small_arrival(at):
-        rows = pl.ds(pl.multiple_of(at * part, part), part)
-        return (
-            remote(upper_ref, fac.at[:, rows], small_send.at[at, 0], small_recv.at[at, 0], {"row": at}),
             remote(
-                map_ref.at[:, half(c)], maps.at[at, :, half(c)], small_send.at[at, 1], small_recv.at[at, 1],
-                {"row": at},
+                map_ref.at[:, half(c)], maps.at[sender, :, half(c)], small_send.at[at, 1],
+                small_recv.at[sender, 1], {"row": at},
             ),
         )
+
+    def share_copy(at, column):
+        rows = pl.ds(pl.multiple_of(at * part + column * piece, piece), piece)
+        return remote(fac.at[:, rows], fac.at[:, rows], share_send.at[at], share_recv.at[at], to_col)
 
     def both_ways(j, first):
         for right in (1, 0):
@@ -452,7 +452,7 @@
     both_ways(0, True)
     x_copy(1).start()
     for at in others():
-        for copy in small_copy(at):
+        for copy in small_copy(at, r):
             copy.start()
     locals_ = [
         pltpu.make_async_copy(slab_ref.at[half(c)], own_slab.at[r, 0], here.at[0]),
@@ -535,13 +535,16 @@
         return carry
 
     lax.fori_loop(0, n_pole, first_pass, 0)
+    for at in others():
+        for copy in small_copy(at, at):
+            copy.wait_recv()
+        share_copy(at, c).start()
     x_copy(1).wait_recv()
     reorder(1, far_slab, r, 1 - c)
     for copy in loads[n_pole:]:
         copy.wait()
     for at in others():
-        for copy in small_arrival(at):
-            copy.wait_recv()
+        share_copy(at, 1 - c).wait_recv()
 
     n_half = n_row // 2
 
@@ -700,7 +703,16 @@
 
     spread[...] = jnp.zeros_like(spread)
     spread[:, pl.ds(pl.multiple_of(r * part, part), part)] = diag_ref[...] * (weight * (1.0 / n_col))
-    wide = [fac[e].astype(jnp.float32) for e in range(fac.shape[0])]
+
+    def times_factor(left, e):
+        return sum(jnp.dot(piece, fac[e], preferred_element_type=jnp.float32) for piece in split(left))
+
+    def factor_times(e, right):
+        dims = (((0,), (0,)), ((), ()))
+        return sum(
+            lax.dot_general(fac[e], piece, dims, preferred_element_type=jnp.float32) for piece in split(right)
+        )
+
     diagonals, crossed = [], {}
 
     def inverse_block(m, n):
@@ -713,9 +725,9 @@
         for m in range(k):
             y_block = inner[k * (k + 1) // 2 + m].T
             for n in range(k):
-                y_block = y_block + precise(inverse_block(m, n), wide[pair_index(k, n)])
+                y_block = y_block + times_factor(inverse_block(m, n), pair_index(k, n))
             crossed[m, k] = -y_block
-            diagonal = diagonal + precise(wide[pair_index(k, m)].T, y_block)
+            diagonal = diagonal + factor_times(pair_index(k, m), y_block)
         diagonals.append(diagonal)
         blocks = diagonal.reshape(n_row, n_pole, depth, width)
         for pole in range(n_pole):
@@ -786,7 +798,8 @@
         copy.wait_send()
     gx_copy.wait_send()
     for at in others():
-        for copy in small_copy(at) + z_copy(at, 0) + gz_copy(at, r):
+        share_copy(at, c).wait_send()
+        for copy in small_copy(at, r) + z_copy(at, 0) + gz_copy(at, r):
             copy.wait_send()
     for j in range(2):
         for right in (1, 0):
@@ -806,6 +819,11 @@
                 @pl.when(block > r)
                 def _():
                     own_copy(block, j, 0).wait_send()
+
+
+def hand_on(columns_ref, diagonal_ref, columns_out, diagonal_out):
+    columns_out[...] = columns_ref[...]
+    diagonal_out[...] = diagonal_ref[...]
 
 
 def fused(window, panels, row_map, panel_root, upper_blocks, diag_inverse, weights, pole_order):
@@ -862,7 +880,7 @@
             pltpu.VMEM((depth, total), f32),
             pltpu.VMEM((depth, total), f32),
             dma((2,)), dma((2,)), dma((2,)), dma((n_col, n_pole)),
-            dma((n_row, 2, 2)), dma((n_row, 2)), dma((n_row, 2)), dma((n_row, 2)),
+            dma((n_row, 2, 2)), dma((n_row, 2)), dma((n_row, 2)), dma((n_row, 2)), dma((n_row,)), dma((n_row,)),
             dma((2, 2)), dma((2, 2)), dma((2, 2)), dma((2, 2)), dma((n_row, 2)), dma((2, n_row, 2)),
             dma((2,)), dma((2,)), dma((2,)), dma((2,)), dma((n_row, 2)), dma((n_row, 2)), dma, dma,
         ],
@@ -871,6 +889,17 @@
         ),
         name="fused",
     )(weights, pole_order, panel_root, rows, slab, row_map, upper_blocks[0], diag_inverse[0])
+    columns, diagonal = pl.pallas_call(
+        hand_on,
+        out_shape=(
+            jax.ShapeDtypeStruct(columns.shape, f32),
+            jax.ShapeDtypeStruct(diagonal.shape, f32),
+        ),
+        in_specs=[vmem, vmem],
+        out_specs=(vmem, vmem),
+        compiler_params=pltpu.CompilerParams(vmem_limit_bytes=8 * 2**20),
+        name="hand_on",
+    )(columns, diagonal)
     return columns[:, None], diagonal
 
 

time: 110 us -> 104 us (0.945)
  Pallas kernels: 105 us -> 101 us
  local copies, waits for them, and re-layouts: 3.48 us -> 1.92 us
    pallas_call x1, Pallas kernels: 105 us -> 99.7 us  [fused(): pl.pallas_call(fused_kernel, out_shape=(jax.ShapeDtypeStruct((NS, share,...]
    unnamed x2 -> x4, local copies, waits for them, and re-layouts: 3.48 us -> 1.92 us
where the time goes in v4:
time: 104 us
  Pallas kernels  101 us (97%)
  local copies, waits for them, and re-layouts  1.92 us (2%)
  between operations  1.3 us (1%)
    pallas_call x1, Pallas kernels, fused(): pl.pallas_call(fused_kernel, out_shape=(jax.ShapeDtypeStruct((NS, share,...  99.7 us

profile of v4, /device:TPU:0, one launch (start us, length us, event | category | flops | bytes accessed | tf_op | source)
XLA Modules:
  0.0 103.9 jit_solution(17796813777664565786)
XLA Ops:
  1.3 99.7 %fused.1 = (f32[3,256,256]{2,1,0:T(8,128)}, f32[3,16,256]{2,1,0:T(8,128)}) custom-call(f32[4]{0:T(128)} %weights_ref.1, s32[1]{0:T(128)S(6)} %copy.11.order_ref, s32[1,3]{1,0:T(1,128)} %root_ref.1, bf16[4,4,256,2048]{3,2,1,0:T(8,128)(2,1)} %bitcast.7, bf16[2048,256]{1,0:T(8,128)(2,1)} %bitcast.8, s32[3,2048]{1,0:T(4,128)} %map_ref.1, ...), custom_call_target="tpu_custom_call" | custom-call | tf_op jit(solution)/shard_map/fused/pallas_call | solution.py:842
  101.0 0.0 copy-start
  101.0 1.1 %copy-done = f32[3,256,256]{2,1,0:T(8,128)S(1)} copy-done((f32[3,256,256]{2,1,0:T(8,128)S(1)}, f32[3,256,256]{2,1,0:T(8,128)}, u32[]{:S(2)}) %copy-start) | copy-done | bytes 786456
  102.1 0.0 copy-start.1
  102.1 0.8 copy-done.1
  102.9 0.9 hand_on.1
Async XLA Ops:
  101.0 1.1 %copy-start = (f32[3,256,256]{2,1,0:T(8,128)S(1)}, f32[3,256,256]{2,1,0:T(8,128)}, u32[]{:S(2)}) copy-start(f32[3,256,256]{2,1,0:T(8,128)} %get-tuple-element.6.columns_ref) | copy-start | bytes 2359300
  102.1 0.8 copy-start.1

commit v5 on v4

--- a/solution.py
+++ b/solution.py
@@ -378,8 +378,8 @@
 
 def fused_kernel(
     weights_ref, order_ref, root_ref, window_ref, slab_ref, map_ref, upper_ref, diag_ref,
-    columns_ref, diagonal_ref,
-    win, own_slab, far_slab, maps, fac, al, y, core_in, y_out, y_out_top, y_in, y_in_top,
+    columns_out, diagonal_ref,
+    columns_ref, out_sem, win, own_slab, far_slab, maps, fac, al, y, core_in, y_out, y_out_top, y_in, y_in_top,
     z_out, z_out_top, z_in, z_in_top, inner, spread, g_all, g_core, g_out, g_out_top, g_in, g_in_top,
     g_sum, gz_out, gz_out_top, gz_in, gz_in_top, g_x, g_last,
     x_send, x_recv, here, win_sem, own_send, own_recv, small_send, small_recv, share_send, share_recv,
@@ -773,6 +773,8 @@
     total = core_in[1, r]
     for k in range(NS):
         columns_ref[k] = total[:, k * width : (k + 1) * width]
+    out_copy = pltpu.make_async_copy(columns_ref, columns_out, out_sem)
+    out_copy.start()
 
     total = g_sum[r]
     for at in others():
@@ -794,6 +796,7 @@
             core_copy(at, h).wait_send()
         for copy in y_copy(at):
             copy.wait_send()
+    out_copy.wait()
     for copy in gy_copies():
         copy.wait_send()
     gx_copy.wait_send()
@@ -846,8 +849,10 @@
             jax.ShapeDtypeStruct((NS, depth, width), f32),
         ),
         in_specs=[smem, smem, smem, hbm, hbm, vmem, vmem, vmem],
-        out_specs=(vmem, vmem),
+        out_specs=(hbm, vmem),
         scratch_shapes=[
+            pltpu.VMEM((NS, share, width), f32),
+            dma,
             pltpu.VMEM((n_col, n_pole, n_row, share, group), bf16),
             pltpu.VMEM((n_row, n_col, group, width), bf16),
             pltpu.VMEM((n_col, group, width), bf16),
@@ -889,15 +894,16 @@
         ),
         name="fused",
     )(weights, pole_order, panel_root, rows, slab, row_map, upper_blocks[0], diag_inverse[0])
+    blocks = [pl.BlockSpec((1, rows_, width), lambda k: (k, 0, 0)) for rows_ in (share, depth)]
     columns, diagonal = pl.pallas_call(
         hand_on,
         out_shape=(
             jax.ShapeDtypeStruct(columns.shape, f32),
             jax.ShapeDtypeStruct(diagonal.shape, f32),
         ),
-        in_specs=[vmem, vmem],
-        out_specs=(vmem, vmem),
-        compiler_params=pltpu.CompilerParams(vmem_limit_bytes=8 * 2**20),
+        grid=(NS,),
+        in_specs=blocks,
+        out_specs=tuple(blocks),
         name="hand_on",
     )(columns, diagonal)
     return columns[:, None], diagonal

time: 104 us -> 104 us (level)
  local copies, waits for them, and re-layouts: 1.92 us -> 0 us
    pallas_call x1, Pallas kernels: 0.93 us -> 2.88 us  [fused(): pl.pallas_call(hand_on, out_shape=(jax.ShapeDtypeStruct(columns.shape, f3...]
    unnamed x4 -> x0, local copies, waits for them, and re-layouts: 1.92 us -> none
where the time goes in v5:
time: 104 us
  Pallas kernels  102 us (98%)
  between operations  1.29 us (1%)
    pallas_call x1, Pallas kernels, fused(): pl.pallas_call(fused_kernel, out_shape=(jax.ShapeDtypeStruct((NS, share,...  99.4 us
    pallas_call x1, Pallas kernels, fused(): pl.pallas_call(hand_on, out_shape=(jax.ShapeDtypeStruct(columns.shape, f3...  2.88 us

profile of v5, /device:TPU:0, one launch (start us, length us, event | category | flops | bytes accessed | tf_op | source)
XLA Modules:
  0.0 103.6 jit_solution(935157135719814849)
XLA Ops:
  1.3 99.4 %fused.1 = (f32[3,256,256]{2,1,0:T(8,128)}, f32[3,16,256]{2,1,0:T(8,128)}) custom-call(f32[4]{0:T(128)} %weights_ref.1, s32[1]{0:T(128)S(6)} %copy.11.order_ref, s32[1,3]{1,0:T(1,128)} %root_ref.1, bf16[4,4,256,2048]{3,2,1,0:T(8,128)(2,1)} %bitcast.7, bf16[2048,256]{1,0:T(8,128)(2,1)} %bitcast.8, s32[3,2048]{1,0:T(4,128)} %map_ref.1, ...), custom_call_target="tpu_custom_call" | custom-call | tf_op jit(solution)/shard_map/fused/pallas_call | solution.py:845
  100.7 2.9 %hand_on.1 = (f32[3,256,256]{2,1,0:T(8,128)}, f32[3,16,256]{2,1,0:T(8,128)}) custom-call(f32[3,256,256]{2,1,0:T(8,128)} %get-tuple-element.6.columns_ref, f32[3,16,256]{2,1,0:T(8,128)} %get-tuple-element.7.diagonal_ref), custom_call_target="tpu_custom_call" | custom-call | tf_op jit(solution)/shard_map/hand_on/pallas_call | solution.py:898
